TPU v7x, 32 devices: a whole 2x2x4 slice. The times are simulated.
32 devices in a mesh: dp: 16 (over z, y, core), mp: 2 (over x).
Axes of the slice: x: 2, y: 2, z: 4, core: 2. Of those that a mesh axis runs over, the one named last changes fastest.
Arguments:
- tokens: bfloat16 [2048, 2048], P('dp', 'mp'), may hold values from -32 to 32
- lengths: int32 [4], replicated, may hold values from 1 to 1536, 2048 in all
- keep_mask: int32 [2048], replicated, may hold values 0 or 1
- routes: int32 [2048, 8], P('dp'), may hold values from 0 to 63, all different within a row; in each aligned block of 128 rows (0 to 127, 128 to 255, ...) at most 32 rows name the same one
- attention_gain: float32 [2048], replicated, may hold values from 0.1 to 1.9
- mixture_gain: float32 [2048], P('mp'), may hold values from 0.1 to 1.9
- query_gain: float32 [128], replicated, may hold values from 0.5 to 8, as said below
- key_gain: float32 [128], replicated, may hold values from 0.5 to 8, as said below
- query_weight: bfloat16 [2048, 2048], P('dp', 'mp'), may hold values from -0.125 to 0.125
- key_weight: bfloat16 [2048, 2048], P('dp', 'mp'), may hold values from -0.125 to 0.125
- value_weight: bfloat16 [2048, 2048], P('dp', 'mp'), may hold values from -0.125 to 0.125
- output_weight: bfloat16 [2048, 2048], P('mp', 'dp'), may hold values from -0.1875 to 0.1875
- router_weight: float32 [2048, 64], P('mp'), may hold values from -0.125 to 0.125
- expert_gate: bfloat16 [16, 2048, 4096], P('dp', None, 'mp'), may hold values from -0.125 to 0.125
- expert_up: bfloat16 [16, 2048, 4096], P('dp', None, 'mp'), may hold values from -0.125 to 0.125
- expert_down: bfloat16 [16, 4096, 2048], P('dp', 'mp'), may hold values from -0.25 to 0.25
Outputs:
- layer_output: bfloat16 [2048, 2048], P('dp', 'mp')
Inputs may be any that keep to these rules, and one draw needn't show every extreme that they name: The lengths sum to 2048; exactly one is 1536. `routes`: each row names 8 different experts. Within each aligned block of 128 rows (the rows of one index of dp) no expert is named by more than 32 rows, a bound that some block reaches. `query_gain`: Positive. `key_gain`: Positive.
All inputs are finite; a program needn't handle non-finite values.
Results may differ from a plain program's by a relative error of at most 0.012.
The roundings to bfloat16 on the way count: a program that leaves them out, or rounds other values in their place, can miss the bound.
Values may be sent and summed in bfloat16 or wider, within the bound.
A program may use at most 128 MiB of HBM per device.

v0:
```python
import jax
import jax.numpy as jnp
from jax import lax
from jax.sharding import PartitionSpec as P

D = 2048
HEAD_DIM = 128
FF = 1024
EXPERTS = 64
TOPK = 8
CAP = 32


EPS = 1e-06
ROPE_BASE = 10000.0
NEG = -1e30


def rope_tables(position):
    halves = HEAD_DIM // 2
    exponent = jnp.arange(halves, dtype=jnp.float32) * (2.0 / HEAD_DIM)
    frequency = jnp.power(jnp.float32(ROPE_BASE), -exponent)
    angle = position.astype(jnp.float32)[:, None] * frequency[None, :]
    cos_table = jnp.cos(angle)
    sin_table = jnp.sin(angle)
    return (jnp.concatenate([cos_table, cos_table], 1), jnp.concatenate([sin_table, sin_table], 1))


def head_prep(projected, head_gain, cos_table, sin_table):
    row_count = projected.shape[0]
    per_head = projected.reshape(row_count, -1, HEAD_DIM)
    normed = (
        per_head * lax.rsqrt(jnp.mean(per_head * per_head, axis=2, keepdims=True) + EPS) * head_gain
    )
    halves = HEAD_DIM // 2
    rotated = jnp.concatenate([-normed[:, :, halves:], normed[:, :, :halves]], 2)
    turned = normed * cos_table[:, None, :] + rotated * sin_table[:, None, :]
    return turned.reshape(row_count, -1).astype(jnp.bfloat16)


def segment_info(lengths, first_row, row_count):
    request_end = jnp.cumsum(lengths)
    request_start = request_end - lengths
    global_row = first_row + jnp.arange(row_count, dtype=jnp.int32)
    segment = jnp.sum((request_end[None, :] <= global_row[:, None]).astype(jnp.int32), axis=1)
    chosen = segment[:, None] == jnp.arange(lengths.shape[0], dtype=jnp.int32)[None, :]
    begin = jnp.sum(jnp.where(chosen, request_start[None, :], 0), axis=1)
    return (segment, global_row - begin, global_row)


def local(
    tokens,
    lengths,
    keep_mask,
    routes,
    attention_gain,
    mixture_gain,
    query_gain,
    key_gain,
    query_weight,
    key_weight,
    value_weight,
    output_weight,
    router_weight,
    expert_gate,
    expert_up,
    expert_down,
):
    tok_rows = tokens.shape[0]
    dp_count = lax.axis_size("dp")
    first_row = lax.axis_index("dp") * tok_rows
    full_tokens = lax.all_gather(tokens, "mp", axis=1, tiled=True)
    xfloat = full_tokens.astype(jnp.float32)
    normed_in = (
        xfloat * lax.rsqrt(jnp.mean(xfloat * xfloat, axis=1, keepdims=True) + EPS) * attention_gain
    ).astype(jnp.bfloat16)
    segment, position, global_row = segment_info(lengths, first_row, tok_rows)
    cos_table, sin_table = rope_tables(position)
    local_width = query_weight.shape[1]
    query_proj = jnp.dot(
        normed_in,
        lax.all_gather(query_weight, "dp", axis=0, tiled=True),
        preferred_element_type=jnp.float32,
    )
    key_proj = jnp.dot(
        normed_in,
        lax.all_gather(key_weight, "dp", axis=0, tiled=True),
        preferred_element_type=jnp.float32,
    )
    value_proj = jnp.dot(
        normed_in,
        lax.all_gather(value_weight, "dp", axis=0, tiled=True),
        preferred_element_type=jnp.float32,
    )
    queries = head_prep(query_proj, query_gain, cos_table, sin_table)
    key_heads = head_prep(key_proj, key_gain, cos_table, sin_table)
    value_heads = value_proj.astype(jnp.bfloat16)
    local_heads = local_width // HEAD_DIM
    query_split = queries.reshape(tok_rows, local_heads, HEAD_DIM)
    seg_low = segment[0]
    seg_high = segment[tok_rows - 1]
    scale = HEAD_DIM ** (-0.5)
    start_state = (
        jnp.full((local_heads, tok_rows), NEG, jnp.float32),
        jnp.zeros((local_heads, tok_rows), jnp.float32),
        jnp.zeros((tok_rows, local_heads, HEAD_DIM), jnp.float32),
    )
    key_piece = lax.all_gather(key_heads, "dp", axis=0, tiled=True)
    value_piece = lax.all_gather(value_heads, "dp", axis=0, tiled=True)
    piece_rows = key_piece.shape[0]
    key_seg, unused_pos, key_row = segment_info(lengths, jnp.int32(0), piece_rows)

    def compute(state_now):
        run_max, run_sum, run_acc = state_now
        key_split = key_piece.reshape(piece_rows, local_heads, HEAD_DIM)
        value_split = value_piece.reshape(piece_rows, local_heads, HEAD_DIM)
        scores = (
            jnp.einsum("thd,shd->hts", query_split, key_split, preferred_element_type=jnp.float32)
            * scale
        )
        visible = (segment[:, None] == key_seg[None, :]) & (
            (keep_mask[None, :] == 1) | (global_row[:, None] == key_row[None, :])
        )
        masked = jnp.where(visible[None], scores, NEG)
        new_max = jnp.maximum(run_max, jnp.max(masked, axis=2))
        factor = jnp.exp(run_max - new_max)
        weights = jnp.where(visible[None], jnp.exp(masked - new_max[:, :, None]), 0.0)
        new_sum = jnp.sum(weights, axis=2)
        mixed = jnp.einsum(
            "hts,shd->thd",
            weights.astype(jnp.bfloat16),
            value_split,
            preferred_element_type=jnp.float32,
        )
        new_acc = run_acc * factor.T[:, :, None] + mixed
        return (new_max, new_sum, new_acc)

    touches = (key_seg[piece_rows - 1] >= seg_low) & (key_seg[0] <= seg_high)
    final_max, final_sum, final_acc = lax.cond(
        touches, compute, lambda state_now: state_now, start_state
    )
    attended = (
        (final_acc / final_sum.T[:, :, None]).reshape(tok_rows, local_width).astype(jnp.bfloat16)
    )
    partial_out = jnp.dot(
        attended,
        lax.all_gather(output_weight, "dp", axis=1, tiled=True),
        preferred_element_type=jnp.float32,
    )
    summed_out = lax.psum_scatter(partial_out, "mp", scatter_dimension=1, tiled=True)
    residual = (tokens.astype(jnp.float32) + summed_out).astype(jnp.bfloat16)
    hfloat = residual.astype(jnp.float32)
    scaled = hfloat * mixture_gain
    partial_logits = jnp.dot(scaled, router_weight, precision=lax.Precision.HIGHEST)
    square_sum, logit_sum = lax.psum((jnp.sum(hfloat * hfloat, axis=1), partial_logits), "mp")
    inverse = lax.rsqrt(square_sum / D + EPS)[:, None]
    mixed_in = (scaled * inverse).astype(jnp.bfloat16)
    logits = logit_sum * inverse
    picked = jnp.take_along_axis(logits, routes, axis=1)
    sigmoid_vals = jax.nn.sigmoid(picked)
    route_weight = sigmoid_vals / jnp.sum(sigmoid_vals, axis=1, keepdims=True)
    onehot = jnp.sum(
        (routes[:, :, None] == jnp.arange(EXPERTS, dtype=jnp.int32)[None, None, :]).astype(
            jnp.int32
        ),
        axis=1,
    )
    before = jnp.cumsum(onehot, axis=0) - onehot
    slot = jnp.take_along_axis(before, routes, axis=1)
    target = routes * CAP + slot
    token_ids = jnp.repeat(jnp.arange(tok_rows, dtype=jnp.int32), TOPK)
    source = jnp.full((EXPERTS * CAP,), tok_rows, jnp.int32).at[target.reshape(-1)].set(token_ids)
    exp_local = EXPERTS // dp_count
    gate_local = expert_gate[0]
    up_local = expert_up[0]
    down_local = expert_down[0]
    unit_count = gate_local.shape[1]
    mp_index = lax.axis_index("mp")
    full_in = lax.all_gather(mixed_in, "mp", axis=1, tiled=True)
    padded = jnp.concatenate([full_in, jnp.zeros((1, full_in.shape[1]), jnp.bfloat16)], 0)
    sending = padded[source].reshape(dp_count, exp_local, CAP, full_in.shape[1])
    rows_in = lax.all_to_all(sending, "dp", split_axis=0, concat_axis=0, tiled=True)
    if unit_count <= FF:
        owners = FF // unit_count
        expert_index = mp_index // owners
        own_rows = lax.dynamic_index_in_dim(rows_in, expert_index, 1, keepdims=False)
        gate_val = jnp.einsum(
            "scd,dh->sch", own_rows, gate_local, preferred_element_type=jnp.float32
        )
        up_val = jnp.einsum("scd,dh->sch", own_rows, up_local, preferred_element_type=jnp.float32)
        hidden = (jax.nn.silu(gate_val) * up_val).astype(jnp.bfloat16)
        own_part = jnp.einsum("sch,hd->scd", hidden, down_local, preferred_element_type=jnp.float32)
        selector = (jnp.arange(exp_local, dtype=jnp.int32) == expert_index).astype(jnp.float32)
        partial_rows = own_part[:, None, :, :] * selector[None, :, None, None]
    else:
        held = unit_count // FF
        first_expert = mp_index * held
        own_rows = lax.dynamic_slice_in_dim(rows_in, first_expert, held, 1)
        gate_val = jnp.einsum(
            "secd,def->secf",
            own_rows,
            gate_local.reshape(gate_local.shape[0], held, FF),
            preferred_element_type=jnp.float32,
        )
        up_val = jnp.einsum(
            "secd,def->secf",
            own_rows,
            up_local.reshape(up_local.shape[0], held, FF),
            preferred_element_type=jnp.float32,
        )
        hidden = (jax.nn.silu(gate_val) * up_val).astype(jnp.bfloat16)
        own_part = jnp.einsum(
            "secf,efd->secd",
            hidden,
            down_local.reshape(held, FF, down_local.shape[1]),
            preferred_element_type=jnp.float32,
        )
        empty_rows = jnp.zeros(
            (rows_in.shape[0], exp_local, rows_in.shape[2], own_part.shape[3]), jnp.float32
        )
        partial_rows = lax.dynamic_update_slice_in_dim(empty_rows, own_part, first_expert, 1)
    summed_rows = lax.psum_scatter(
        partial_rows.astype(jnp.bfloat16), "mp", scatter_dimension=3, tiled=True
    )
    returned = lax.all_to_all(summed_rows, "dp", split_axis=0, concat_axis=0, tiled=True)
    flat = returned.reshape(EXPERTS * CAP, local_width)
    gathered = flat[target]
    mixture = jnp.sum(gathered.astype(jnp.float32) * route_weight[:, :, None], axis=1)
    return (hfloat + mixture).astype(jnp.bfloat16)


def solution(mesh):
    return jax.shard_map(
        local,
        mesh=mesh,
        in_specs=(
            P("dp", "mp"),
            P(),
            P(),
            P("dp", None),
            P(),
            P("mp"),
            P(),
            P(),
            P("dp", "mp"),
            P("dp", "mp"),
            P("dp", "mp"),
            P("mp", "dp"),
            P("mp", None),
            P("dp", None, "mp"),
            P("dp", None, "mp"),
            P("dp", "mp", None),
        ),
        out_specs=P("dp", "mp"),
        check_vma=False,
    )
```

profile of v0, /device:TPU:0, one launch (start us, length us, event | category | flops | bytes accessed | tf_op | source)
XLA Modules:
  0.0 797.4 jit_solution(14257861319533035457)
XLA Ops:
  10.9 10.2 %all_gather.24 = bf16[128,2048]{1,0:T(8,128)(2,1)S(1)} all-gather(bf16[128,1024]{1,0:T(8,128)(2,1)} %param.18), channel_id=1, replica_groups=mesh['dp'=16,'mp'=2] {'mp'}, dimensions={1}, use_global_device_ids=true | all-gather | bytes 786432 | tf_op jit(solution)/shard_map/all_gather | solution.py:72
  22.0 41.0 %all-gather.9.cloned.1.call-done = bf16[2048,1024]{1,0:T(8,128)(2,1)} async-done(((bf16[128,1024]{1,0:T(8,128)(2,1)}), bf16[2048,1024]{1,0:T(8,128)(2,1)}) %all-gather.9.cloned.1.call-update) | async-done | bytes 4194320 | tf_op jit(solution)/shard_map/all_gather | solution.py:87
  66.5 47.8 %all-gather.7.cloned.1.call-done = bf16[2048,1024]{1,0:T(8,128)(2,1)} async-done(((bf16[128,1024]{1,0:T(8,128)(2,1)}), bf16[2048,1024]{1,0:T(8,128)(2,1)}) %all-gather.7.cloned.1.call-update) | async-done | bytes 4194320 | tf_op jit(solution)/shard_map/all_gather | solution.py:82
  120.6 44.8 %all-gather.13.cloned.1.call-done = bf16[2048,1024]{1,0:T(8,128)(2,1)} async-done(((bf16[128,1024]{1,0:T(8,128)(2,1)}), bf16[2048,1024]{1,0:T(8,128)(2,1)}) %all-gather.13.cloned.1.call-update) | async-done | bytes 4194320 | tf_op jit(solution)/shard_map/all_gather | solution.py:92
  165.5 3.6 convolution_convert_fusion
  173.1 43.5 %all-gather.11.cloned.1.call-done = bf16[2048,1024]{1,0:T(8,128)(2,1)} async-done(((bf16[128,1024]{1,0:T(8,128)(2,1)}), bf16[2048,1024]{1,0:T(8,128)(2,1)}) %all-gather.11.cloned.1.call-update) | async-done | bytes 4194320 | tf_op jit(solution)/shard_map/all_gather | solution.py:108
  216.6 51.1 %all-gather.15.cloned.1.call-done = bf16[2048,1024]{1,0:T(8,128)(2,1)} async-done(((bf16[128,1024]{1,0:T(8,128)(2,1)}), bf16[2048,1024]{1,0:T(8,128)(2,1)}) %all-gather.15.cloned.1.call-update) | async-done | bytes 4194320 | tf_op jit(solution)/shard_map/all_gather | solution.py:109
  267.7 16.4 %conditional.1 = (f32[8,128]{1,0:T(8,128)S(1)}, f32[128,8,128]{0,2,1:T(8,128)S(1)}) conditional(s32[]{:T(128)} %bitcast.4, () %tuple.13, (s32[128]{0:T(128)S(1)}, s32[2048]{0:T(1024)S(1)}, s32[2048]{0:T(1024)S(1)}, s32[]{:T(128)}, s32[128]{0:T(128)S(1)}, /*index=5*/s32[2048]{0:T(1024)S(1)}, bf16[128,1024]{1,0:T(8,128)(2,1)S(1)}, ...), branch_computations={%region_7.8_spmd, %region_8.11_spmd} | conditional | flops 1102187648 | bytes 86833224 | solution.py:139
  268.1 4.6 fusion
  272.7 3.2 copy-done.2
  275.9 3.3 fusion.19
  279.4 4.7 fusion.2
  284.2 37.2 %all-gather.17.cloned.1.call-done = bf16[1024,2048]{1,0:T(8,128)(2,1)} async-done(((bf16[1024,128]{1,0:T(8,128)(2,1)}), bf16[1024,2048]{1,0:T(8,128)(2,1)}) %all-gather.17.cloned.1.call-update) | async-done | bytes 4194320 | tf_op jit(solution)/shard_map/all_gather | solution.py:147
  321.4 3.9 fusion.73
  325.9 7.1 gather_fusion.2
  333.5 4.3 scatter_custom_fusion
  337.8 6.2 reduce-scatter.3.cloned.1.call-done
  345.9 7.3 all-reduce.1
  353.3 7.0 all_gather.31
  360.4 11.0 %gather_fusion = bf16[2048,2048]{1,0:T(8,128)(2,1)} fusion(bf16[129,2048]{1,0:T(8,128)(2,1)S(1)} %concatenate.19, s32[2048]{0:T(1024)S(1)} %fusion.62), kind=kCustom, calls=%fused_computation | custom fusion | bytes 16785408 | tf_op jit(solution)/shard_map/gather | solution.py:181
  371.4 5.9 all-to-all-start
  377.4 14.4 %reshape_squeeze.10 = bf16[2048,2,1024]{2,1,0:T(2,128)(2,1)} reshape(bf16[1,2048,2048]{2,1,0:T(8,128)(2,1)} %param.32) | data formatting | bytes 16777216 | tf_op jit(solution)/shard_map/reshape;squeeze | solution.py:208
  391.8 14.5 %reshape_squeeze.9 = bf16[2048,2,1024]{2,1,0:T(2,128)(2,1)} reshape(bf16[1,2048,2048]{2,1,0:T(8,128)(2,1)} %param.31) | data formatting | bytes 16777216 | tf_op jit(solution)/shard_map/reshape;squeeze | solution.py:202
  406.3 121.7 %all-to-all-done = bf16[16,4,32,2048]{3,2,1,0:T(8,128)(2,1)} async-done(((bf16[16,4,32,2048]{3,2,1,0:T(8,128)(2,1)}), bf16[16,4,32,2048]{3,2,1,0:T(8,128)(2,1)}, u32[]{:S(2)}, u32[]{:S(2)}) %all-to-all-start) | async-done | bytes 8388640 | tf_op jit(solution)/shard_map/all_to_all | solution.py:182
  528.0 11.3 %fusion.29 = f32[2,16,32,1024]{3,2,1,0:T(8,128)} fusion(bf16[2048,2,1024,1]{2,1,0,3:T(2,128)(2,1)} %bitcast.132, bf16[16,4,32,2048]{3,2,1,0:T(8,128)(2,1)} %all-to-all-done, s32[]{:T(128)S(6)} %select_n.52), kind=kOutput, calls=%fused_computation.32 | convolution fusion | flops 4294967296 | bytes 16777220 | tf_op jit(solution)/shard_map/secd,def->secf/dot_general | solution.py:205
  539.3 20.3 %convolution_bitcast_fusion = bf16[16,2,32,2048]{3,2,0,1:T(8,128)(2,1)} fusion(bf16[2,1024,2048,1]{2,1,3,0:T(8,128)(2,1)} %bitcast.147, f32[2,16,32,1024]{3,2,1,0:T(8,128)} %fusion.29, bf16[2048,2,1024,1]{2,1,0,3:T(2,128)(2,1)} %bitcast.131, bf16[16,4,32,2048]{3,2,1,0:T(8,128)(2,1)} %all-to-all-done, s32[]{:T(128)S(6)} %select_n.52), kind=kOutput, calls=%fused_computation.37 | convolution fusion | flops 8596226048 | bytes 29360132 | tf_op jit(solution)/shard_map/secf,efd->secd/dot_general | solution.py:212
  559.6 4.3 broadcast_in_dim.70
  566.2 131.2 %reduce-scatter.5.cloned.1.call-done = bf16[16,4,32,1024]{3,2,1,0:T(8,128)(2,1)} async-done(((bf16[16,4,32,2048]{3,2,1,0:T(8,128)(2,1)}), bf16[16,4,32,1024]{3,2,1,0:T(8,128)(2,1)}) %reduce-scatter.5.cloned.1.call-update) | async-done | bytes 4194320 | tf_op jit(solution)/shard_map/reduce_scatter | solution.py:222
  697.4 5.7 all-to-all-start.1
  703.3 7.0 gather_fusion.3
  710.6 70.1 %all-to-all-done.1 = bf16[16,4,32,1024]{3,2,1,0:T(8,128)(2,1)} async-done(((bf16[16,4,32,1024]{3,2,1,0:T(8,128)(2,1)}), bf16[16,4,32,1024]{3,2,1,0:T(8,128)(2,1)}, u32[]{:S(2)}, u32[]{:S(2)}) %all-to-all-start.1) | async-done | bytes 4194336 | tf_op jit(solution)/shard_map/all_to_all | solution.py:225
  780.7 7.7 gather_fusion.1
  (114 shorter events, 24.8 us)
Async XLA Ops:
  6.5 338.7 %copy-start = (f32[1024,64]{0,1:T(8,128)S(1)}, f32[1024,64]{0,1:T(8,128)}, u32[]{:S(2)}) copy-start(f32[1024,64]{0,1:T(8,128)} %param.30) | copy-start | bytes 786436
  6.5 56.4 %all-gather.9.cloned.1.call-start = ((), (), s32[]{:S(2)}) async-start(), calls=%async_computation.5 | async-start | bytes 4456448 | tf_op jit(solution)/shard_map/all_gather | solution.py:87
  7.3 107.0 %all-gather.7.cloned.1.call-start = ((), (), s32[]{:S(2)}) async-start(), calls=%async_computation.4 | async-start | bytes 4456448 | tf_op jit(solution)/shard_map/all_gather | solution.py:82
  8.0 157.5 %all-gather.13.cloned.1.call-start = ((), (), s32[]{:S(2)}) async-start(), calls=%async_computation.7 | async-start | bytes 4456448 | tf_op jit(solution)/shard_map/all_gather | solution.py:92
  8.7 207.8 %all-gather.11.cloned.1.call-start = ((), (), s32[]{:S(2)}) async-start(), calls=%async_computation.6 | async-start | bytes 4456448 | tf_op jit(solution)/shard_map/all_gather | solution.py:108
  10.9 103.3 %copy-start.6 = (f32[2048]{0:T(1024)S(1)}, f32[2048]{0:T(1024)}, u32[]{:S(2)}) copy-start(f32[2048]{0:T(1024)} %param.22) | copy-start | bytes 24580
  65.9 51.7 %copy-start.9 = (f32[128]{0:T(128)S(1)}, f32[128]{0:T(128)}, u32[]{:S(2)}) copy-start(f32[128]{0:T(128)} %param.25) | copy-start | bytes 1540
  66.3 51.6 %copy-start.10 = (f32[128]{0:T(128)S(1)}, f32[128]{0:T(128)}, u32[]{:S(2)}) copy-start(f32[128]{0:T(128)} %param.24) | copy-start | bytes 1540
  119.3 148.4 %copy-start.8 = (s32[2048]{0:T(1024)S(1)}, s32[2048]{0:T(1024)}, u32[]{:S(2)}) copy-start(s32[2048]{0:T(1024)} %param.20) | copy-start | bytes 24580
  120.6 147.1 %all-gather.15.cloned.1.call-start = ((), (), s32[]{:S(2)}) async-start(), calls=%async_computation.8 | async-start | bytes 4456448 | tf_op jit(solution)/shard_map/all_gather | solution.py:109
  169.1 152.3 %all-gather.17.cloned.1.call-start = ((), (), s32[]{:S(2)}) async-start(), calls=%async_computation.9 | async-start | bytes 4456448 | tf_op jit(solution)/shard_map/all_gather | solution.py:147
  169.7 174.3 %reduce-scatter.3.cloned.1.call-start = ((), (), s32[]{:S(2)}) async-start(), calls=%async_computation.10 | async-start | bytes 1572864 | tf_op jit(solution)/shard_map/reduce_scatter | solution.py:150
  268.1 7.8 copy-start.11
  272.7 3.2 copy-start.2
  284.1 41.2 %copy-start.5 = (s32[128,8]{0,1:T(8,128)S(1)}, s32[128,8]{0,1:T(8,128)}, u32[]{:S(2)}) copy-start(s32[128,8]{0,1:T(8,128)} %param.21) | copy-start | bytes 12292
  325.9 18.1 %copy-start.4 = (bf16[128,1024]{1,0:T(8,128)(2,1)S(1)}, bf16[128,1024]{1,0:T(8,128)(2,1)}, u32[]{:S(2)}) copy-start(bf16[128,1024]{1,0:T(8,128)(2,1)} %param.18) | copy-start | bytes 786436
  325.9 19.3 %copy-start.7 = (f32[1024]{0:T(1024)S(1)}, f32[1024]{0:T(1024)}, u32[]{:S(2)}) copy-start(f32[1024]{0:T(1024)} %param.23) | copy-start | bytes 12292
  371.4 156.6 %all-to-all-start = ((bf16[16,4,32,2048]{3,2,1,0:T(8,128)(2,1)}), bf16[16,4,32,2048]{3,2,1,0:T(8,128)(2,1)}, u32[]{:S(2)}, u32[]{:S(2)}) async-start(bf16[16,4,32,2048]{3,2,1,0:T(8,128)(2,1)} %bitcast.130), calls=%async_computation.1 | async-start | bytes 16777216 | tf_op jit(solution)/shard_map/all_to_all | solution.py:182
  377.3 320.1 %reduce-scatter.5.cloned.1.call-start = ((), (), s32[]{:S(2)}) async-start(), calls=%async_computation.11 | async-start | bytes 12582912 | tf_op jit(solution)/shard_map/reduce_scatter | solution.py:222
  559.6 4.3 copy-start.3
  697.4 83.3 %all-to-all-start.1 = ((bf16[16,4,32,1024]{3,2,1,0:T(8,128)(2,1)}), bf16[16,4,32,1024]{3,2,1,0:T(8,128)(2,1)}, u32[]{:S(2)}, u32[]{:S(2)}) async-start(bf16[16,4,32,1024]{3,2,1,0:T(8,128)(2,1)} %reduce-scatter.5.cloned.1.call-done), calls=%async_computation.3 | async-start | bytes 8388608 | tf_op jit(solution)/shard_map/all_to_all | solution.py:225
  780.7 9.8 %copy-start.1 = (f32[1024,64]{0,1:T(8,128)S(1)}, f32[1024,64]{0,1:T(8,128)}, u32[]{:S(2)}) copy-start(f32[1024,64]{0,1:T(8,128)} %param.30) | copy-start | bytes 786436
Sparse Core Ops, SparseCore 0:
  9.5 53.4 all-gather.8
  65.1 49.0 all-gather.6
  116.4 49.0 all-gather.12
  167.5 49.0 all-gather.10
  218.6 49.0 all-gather.14
  269.7 51.7 all-gather.16
  325.5 18.4 reduce-scatter.2
  566.3 131.0 reduce-scatter.4
where the time goes:
time: 813 us; the launch traced here: 797 us
  waiting for transfers between devices  597 us (73%)
  local copies, waits for them, and re-layouts  79.6 us (10%)
  matrix products  53.6 us (7%)
  blocking collectives  24.5 us (3%)
  between operations  16.5 us (2%)
  other arithmetic  14 us (2%)
  starting transfers between devices  11.8 us (1%)
    reduce_scatter x1, waiting for transfers between devices, local(): lax.psum_scatter(partial_rows.astype(jnp.bfloat16), 'mp', scatter_dimensi...  131 us
    all_to_all x1, waiting for transfers between devices, local(): lax.all_to_all(sending, 'dp', split_axis=0, concat_axis=0, tiled=True)  122 us
    all_to_all x1, waiting for transfers between devices, local(): lax.all_to_all(summed_rows, 'dp', split_axis=0, concat_axis=0, tiled=True)  70.1 us
    all_gather x1, waiting for transfers between devices, local(): value_piece = lax.all_gather(value_heads, 'dp', axis=0, tiled=True)  51.1 us
    all_gather x1, waiting for transfers between devices, local(): lax.all_gather(query_weight, 'dp', axis=0, tiled=True)  47.8 us
    all_gather x1, waiting for transfers between devices, local(): lax.all_gather(value_weight, 'dp', axis=0, tiled=True)  44.8 us
    all_gather x1, waiting for transfers between devices, local(): key_piece = lax.all_gather(key_heads, 'dp', axis=0, tiled=True)  43.5 us
    all_gather x1, waiting for transfers between devices, local(): lax.all_gather(key_weight, 'dp', axis=0, tiled=True)  41 us
  transfers between devices with their start and end apart: 10, of which 10 were waited for; matrix products, arithmetic and copies ran while one was open for 10% of the time, Pallas kernels for 0%

commit v1 on v0

v1 whole, which is shorter than its diff:
```python
import jax
import jax.numpy as jnp
from jax import lax
from jax.sharding import PartitionSpec as P

D = 2048
HEAD_DIM = 128
FF = 1024
EXPERTS = 64
TOPK = 8
CAP = 32


EPS = 1e-06
ROPE_BASE = 10000.0
NEG = -1e30


def rope_tables(position):
    halves = HEAD_DIM // 2
    exponent = jnp.arange(halves, dtype=jnp.float32) * (2.0 / HEAD_DIM)
    frequency = jnp.power(jnp.float32(ROPE_BASE), -exponent)
    angle = position.astype(jnp.float32)[:, None] * frequency[None, :]
    cos_table = jnp.cos(angle)
    sin_table = jnp.sin(angle)
    return (jnp.concatenate([cos_table, cos_table], 1), jnp.concatenate([sin_table, sin_table], 1))


def head_prep(projected, head_gain, cos_table, sin_table):
    row_count = projected.shape[0]
    per_head = projected.reshape(row_count, -1, HEAD_DIM)
    normed = (
        per_head * lax.rsqrt(jnp.mean(per_head * per_head, axis=2, keepdims=True) + EPS) * head_gain
    )
    halves = HEAD_DIM // 2
    rotated = jnp.concatenate([-normed[:, :, halves:], normed[:, :, :halves]], 2)
    turned = normed * cos_table[:, None, :] + rotated * sin_table[:, None, :]
    return turned.reshape(row_count, -1).astype(jnp.bfloat16)


def segment_info(lengths, global_row):
    request_end = jnp.cumsum(lengths)
    request_start = request_end - lengths
    segment = jnp.sum((request_end[None, :] <= global_row[:, None]).astype(jnp.int32), axis=1)
    chosen = segment[:, None] == jnp.arange(lengths.shape[0], dtype=jnp.int32)[None, :]
    begin = jnp.sum(jnp.where(chosen, request_start[None, :], 0), axis=1)
    return (segment, global_row - begin)


def gather_tokens(block):
    return lax.all_gather(block, "dp", axis=0, tiled=True)


def attention(queries, keys, values, query_seg, query_row, key_seg, key_row, keep_mask):
    scale = HEAD_DIM ** (-0.5)
    scores = (
        lax.dot_general(
            queries, keys, (((1,), (1,)), ((), ())), preferred_element_type=jnp.float32
        )
        * scale
    )
    visible = (query_seg[:, None] == key_seg[None, :]) & (
        (keep_mask[None, :] == 1) | (query_row[:, None] == key_row[None, :])
    )
    masked = jnp.where(visible, scores, NEG)
    top = jnp.max(masked, axis=1, keepdims=True)
    weights = jnp.where(visible, jnp.exp(masked - top), 0.0)
    totals = jnp.sum(weights, axis=1, keepdims=True)
    mixed = jnp.dot(weights.astype(jnp.bfloat16), values, preferred_element_type=jnp.float32)
    return (mixed / totals).astype(jnp.bfloat16)


def local(
    tokens,
    lengths,
    keep_mask,
    routes,
    attention_gain,
    mixture_gain,
    query_gain,
    key_gain,
    query_weight,
    key_weight,
    value_weight,
    output_weight,
    router_weight,
    expert_gate,
    expert_up,
    expert_down,
):
    tok_rows = tokens.shape[0]
    dp_count = lax.axis_size("dp")
    dp_index = lax.axis_index("dp")
    mp_index = lax.axis_index("mp")
    local_width = query_weight.shape[1]
    local_heads = local_width // HEAD_DIM
    share = dp_count // local_heads
    part = dp_index % share
    total_rows = tok_rows * dp_count

    weight_rows = query_weight.shape[0]
    packed = jnp.stack([query_weight, key_weight, value_weight]).reshape(
        3, weight_rows, local_heads, HEAD_DIM
    )
    packed = packed.transpose(2, 1, 0, 3).reshape(local_heads, weight_rows, 3 * HEAD_DIM)
    packed = jnp.repeat(packed, share, axis=0)
    head_weight = lax.all_to_all(packed, "dp", split_axis=0, concat_axis=0, tiled=True)
    head_weight = head_weight.reshape(dp_count * weight_rows, 3 * HEAD_DIM)

    full_tokens = lax.all_gather(tokens, "mp", axis=1, tiled=True)
    xfloat = full_tokens.astype(jnp.float32)
    normed_in = (
        xfloat * lax.rsqrt(jnp.mean(xfloat * xfloat, axis=1, keepdims=True) + EPS) * attention_gain
    ).astype(jnp.bfloat16)
    all_in = gather_tokens(normed_in)
    all_output_weight = lax.all_gather(output_weight, "dp", axis=1, tiled=True)

    key_row = jnp.arange(total_rows, dtype=jnp.int32)
    key_seg, key_pos = segment_info(lengths, key_row)
    cos_table, sin_table = rope_tables(key_pos)

    def own(array):
        split = array.reshape((local_heads, share, tok_rows) + array.shape[1:])
        taken = lax.dynamic_index_in_dim(split, part, 1, keepdims=False)
        return taken.reshape((local_heads * tok_rows,) + array.shape[1:])

    projected = jnp.dot(all_in, head_weight, preferred_element_type=jnp.float32)
    queries = head_prep(
        own(projected[:, :HEAD_DIM]), query_gain, own(cos_table), own(sin_table)
    )
    keys = head_prep(projected[:, HEAD_DIM : 2 * HEAD_DIM], key_gain, cos_table, sin_table)
    values = projected[:, 2 * HEAD_DIM :].astype(jnp.bfloat16)
    attended = attention(
        queries, keys, values, own(key_seg), own(key_row), key_seg, key_row, keep_mask
    )
    groups = [[head * share + p for head in range(local_heads)] for p in range(share)]
    attended = lax.all_to_all(
        attended.reshape(local_heads, tok_rows, HEAD_DIM),
        "dp",
        split_axis=0,
        concat_axis=0,
        tiled=True,
        axis_index_groups=groups,
    )
    attended = attended.transpose(1, 0, 2).reshape(tok_rows, local_width)
    partial_out = jnp.dot(attended, all_output_weight, preferred_element_type=jnp.float32)
    summed_out = lax.psum_scatter(partial_out, "mp", scatter_dimension=1, tiled=True)
    residual = (tokens.astype(jnp.float32) + summed_out).astype(jnp.bfloat16)
    hfloat = residual.astype(jnp.float32)
    scaled = hfloat * mixture_gain
    partial_logits = jnp.dot(scaled, router_weight, precision=lax.Precision.HIGHEST)
    square_sum, logit_sum = lax.psum((jnp.sum(hfloat * hfloat, axis=1), partial_logits), "mp")
    inverse = lax.rsqrt(square_sum / D + EPS)[:, None]
    mixed_in = (scaled * inverse).astype(jnp.bfloat16)
    logits = logit_sum * inverse

    experts = jnp.arange(EXPERTS, dtype=jnp.int32)
    named = jnp.any(routes[None, :, :] == experts[:, None, None], axis=2)
    named_float = named.astype(jnp.float32)
    sigmoid_vals = jax.nn.sigmoid(logits).T * named_float
    route_weight = sigmoid_vals / jnp.sum(sigmoid_vals, axis=0, keepdims=True)
    ids = jnp.arange(tok_rows, dtype=jnp.int32)
    earlier = (ids[:, None] < ids[None, :]).astype(jnp.bfloat16)
    before = jnp.dot(named.astype(jnp.bfloat16), earlier, preferred_element_type=jnp.float32)
    place = jnp.where(named, before.astype(jnp.int32), -1)

    exp_local = EXPERTS // dp_count
    gate_local = expert_gate[0]
    up_local = expert_up[0]
    down_local = expert_down[0]
    unit_count = gate_local.shape[1]
    held = max(1, unit_count // FF)
    units = unit_count // held
    first_expert = (mp_index * unit_count) // FF

    def mine(table):
        split = table.reshape(dp_count, exp_local, tok_rows)
        return lax.dynamic_slice_in_dim(split, first_expert, held, 1)

    slots = jnp.arange(CAP, dtype=jnp.int32)
    chosen = mine(place)[:, :, None, :] == slots[None, None, :, None]
    select = chosen.astype(jnp.bfloat16).reshape(dp_count * held * CAP, tok_rows)
    full_in = lax.all_gather(mixed_in, "mp", axis=1, tiled=True)
    sending = jnp.dot(select, full_in, preferred_element_type=jnp.float32).astype(jnp.bfloat16)
    rows_in = lax.all_to_all(
        sending.reshape(dp_count, held, CAP, D), "dp", split_axis=0, concat_axis=0, tiled=True
    )
    outs = []
    for index in range(held):
        rows = rows_in[:, index].reshape(dp_count * CAP, D)
        low, high = index * units, (index + 1) * units
        gate_val = jnp.dot(rows, gate_local[:, low:high], preferred_element_type=jnp.float32)
        up_val = jnp.dot(rows, up_local[:, low:high], preferred_element_type=jnp.float32)
        hidden = (jax.nn.silu(gate_val) * up_val).astype(jnp.bfloat16)
        out = jnp.dot(hidden, down_local[low:high], preferred_element_type=jnp.float32)
        outs.append(out.astype(jnp.bfloat16).reshape(dp_count, CAP, D))
    returned = lax.all_to_all(
        jnp.stack(outs, axis=1), "dp", split_axis=0, concat_axis=0, tiled=True
    ).reshape(dp_count * held * CAP, D)
    spread = jnp.where(chosen, mine(route_weight)[:, :, None, :], 0.0)
    spread = spread.reshape(dp_count * held * CAP, tok_rows)
    spread_high = spread.astype(jnp.bfloat16)
    spread_mid = (spread - spread_high.astype(jnp.float32)).astype(jnp.bfloat16)
    contract = (((0,), (0,)), ((), ()))
    mixture = lax.dot_general(
        spread_high, returned, contract, preferred_element_type=jnp.float32
    ) + lax.dot_general(spread_mid, returned, contract, preferred_element_type=jnp.float32)
    mixture = lax.psum_scatter(mixture, "mp", scatter_dimension=1, tiled=True)
    return (hfloat + mixture).astype(jnp.bfloat16)


def solution(mesh):
    return jax.shard_map(
        local,
        mesh=mesh,
        in_specs=(
            P("dp", "mp"),
            P(),
            P(),
            P("dp", None),
            P(),
            P("mp"),
            P(),
            P(),
            P("dp", "mp"),
            P("dp", "mp"),
            P("dp", "mp"),
            P("mp", "dp"),
            P("mp", None),
            P("dp", None, "mp"),
            P("dp", None, "mp"),
            P("dp", "mp", None),
        ),
        out_specs=P("dp", "mp"),
        check_vma=False,
    )
```

time: 813 us -> 494 us (0.61); the launches traced: 797 us -> 489 us
  waiting for transfers between devices: 597 us -> 241 us
  blocking collectives: 24.5 us -> 123 us
  local copies, waits for them, and re-layouts: 79.6 us -> 15.8 us
  other arithmetic: 14 us -> 24.8 us
    all_gather x6 -> x2, waiting for transfers between devices: 265 us -> 67.9 us  [the longest x1 43.2 us: gather_tokens(): return lax.all_gather(block, 'dp', axis=0, tiled=True)]
    all_to_all x0 -> x1, blocking collectives: none -> 98.4 us  [local(): lax.all_to_all(sending.reshape(dp_count, held, CAP, D), 'dp', split_axis=...]
    reduce_scatter x1, waiting for transfers between devices: 131 us -> 35.4 us  [local(): mixture = lax.psum_scatter(mixture, 'mp', scatter_dimension=1, tiled=True)]
    all_to_all x2 -> x3, waiting for transfers between devices: 192 us -> 117 us  [the longest x1 77.5 us: local(): lax.all_to_all(jnp.stack(outs, axis=1), 'dp', split_axis=0, concat_axis=0...]
    gather x10 -> x0, local copies, waits for them, and re-layouts: 33.3 us -> none  [the longest x1 11 us: local(): sending = padded[source].reshape(dp_count, exp_local, CAP, full_in.shape[1])]
    another operation x2 -> x0, local copies, waits for them, and re-layouts: 28.9 us -> none  [the longest x1 14.5 us: local(): gate_local.reshape(gate_local.shape[0], held, FF)]
    reduce_scatter x1, waiting for transfers between devices: 6.15 us -> 20.3 us  [local(): lax.psum_scatter(partial_out, 'mp', scatter_dimension=1, tiled=True)]
    unnamed x22 -> x38, local copies, waits for them, and re-layouts: 0.25 us -> 9.08 us
  transfers between devices with their start and end apart: 10 -> 7, of which waited for: 10 -> 6; matrix products, arithmetic and copies ran while one was open for 10% -> 8% of each run, Pallas kernels for 0% -> 0%
where the time goes in v1:
time: 494 us; the launch traced here: 489 us
  waiting for transfers between devices  241 us (49%)
  blocking collectives  123 us (25%)
  matrix products  54.4 us (11%)
  other arithmetic  24.8 us (5%)
  local copies, waits for them, and re-layouts  15.8 us (3%)
  starting transfers between devices  15.2 us (3%)
  between operations  14 us (3%)
    all_to_all x1, blocking collectives, local(): lax.all_to_all(sending.reshape(dp_count, held, CAP, D), 'dp', split_axis=...  98.4 us
    all_to_all x1, waiting for transfers between devices, local(): lax.all_to_all(jnp.stack(outs, axis=1), 'dp', split_axis=0, concat_axis=0...  77.5 us
    all_gather x1, waiting for transfers between devices, gather_tokens(): return lax.all_gather(block, 'dp', axis=0, tiled=True)  43.2 us
    all_to_all x1, waiting for transfers between devices, local(): lax.all_to_all(packed, 'dp', split_axis=0, concat_axis=0, tiled=True)  39.4 us
    reduce_scatter x1, waiting for transfers between devices, local(): mixture = lax.psum_scatter(mixture, 'mp', scatter_dimension=1, tiled=True)  35.4 us
    all_gather x1, waiting for transfers between devices, local(): all_output_weight = lax.all_gather(output_weight, 'dp', axis=1, tiled=True)  24.8 us
    dot_general x2, matrix products, local(): jnp.dot(hidden, down_local[low:high], preferred_element_type=jnp.float32)  20.5 us
    reduce_scatter x1, waiting for transfers between devices, local(): lax.psum_scatter(partial_out, 'mp', scatter_dimension=1, tiled=True)  20.3 us
  transfers between devices with their start and end apart: 7, of which 6 were waited for; matrix products, arithmetic and copies ran while one was open for 8% of the time, Pallas kernels for 0%

profile of v1, /device:TPU:0, one launch (start us, length us, event | category | flops | bytes accessed | tf_op | source)
XLA Modules:
  0.0 488.6 jit_solution(367880626133548728)
XLA Ops:
  6.5 10.3 %all_gather.12 = bf16[128,2048]{1,0:T(8,128)(2,1)S(1)} all-gather(bf16[128,1024]{1,0:T(8,128)(2,1)} %param.16), channel_id=1, replica_groups=mesh['dp'=16,'mp'=2] {'mp'}, dimensions={1}, use_global_device_ids=true | all-gather | bytes 786432 | tf_op jit(solution)/shard_map/all_gather | solution.py:110
  17.0 1.7 fusion.35
  24.0 6.2 %all-to-all-start = ((bf16[16,128,384]{2,1,0:T(8,128)(2,1)}), bf16[16,128,384]{2,1,0:T(8,128)(2,1)}, u32[]{:S(2)}, u32[]{:S(2)}) async-start(bf16[16,128,384]{2,1,0:T(8,128)(2,1)} %bitcast.10), calls=%async_computation | async-start | bytes 3145728 | tf_op jit(solution)/shard_map/all_to_all | solution.py:107
  31.5 3.7 multiply_cosine_fusion
  35.2 3.0 multiply_sine_fusion.1
  38.2 39.4 %all-to-all-done = bf16[16,128,384]{2,1,0:T(8,128)(2,1)} async-done(((bf16[16,128,384]{2,1,0:T(8,128)(2,1)}), bf16[16,128,384]{2,1,0:T(8,128)(2,1)}, u32[]{:S(2)}, u32[]{:S(2)}) %all-to-all-start) | async-done | bytes 1572896 | tf_op jit(solution)/shard_map/all_to_all | solution.py:107
  77.6 43.2 %all-gather.3.cloned.1.call-done = bf16[2048,2048]{1,0:T(8,128)(2,1)} async-done(((bf16[128,2048]{1,0:T(8,128)(2,1)}), bf16[2048,2048]{1,0:T(8,128)(2,1)}) %all-gather.3.cloned.1.call-update) | async-done | bytes 8388624 | tf_op jit(solution)/shard_map/all_gather | solution.py:51
  120.7 6.4 %fusion.88 = f32[2048,384]{0,1:T(8,128)S(1)} fusion(bf16[2048,2048]{1,0:T(8,128)(2,1)} %all-gather.3.cloned.1.call-done, bf16[2048,384]{1,0:T(8,128)(2,1)} %bitcast.11), kind=kOutput, calls=%fused_computation.130 | convolution fusion | flops 3221225472 | bytes 13107200 | tf_op jit(solution)/shard_map/dot_general | solution.py:127
  130.0 1.9 reshape.358
  131.9 1.7 constant_dynamic-slice_fusion.2
  136.6 3.4 fusion.2
  140.1 5.0 %fusion.3 = f32[1024]{0:T(1024)S(1)} fusion(f32[1024,2048]{1,0:T(8,128)S(1)} %get-tuple-element.24, f32[1024]{0:T(1024)S(1)} %get-tuple-element.23, s32[1024]{0:T(1024)S(1)} %bitcast.112, pred[2048]{0:T(1024)(128)(4,1)S(1)} %broadcast_compare_fusion, s32[2048]{0:T(1024)S(1)} %convert_reduce_fusion, s32[1024]{0:T(1024)S(1)} %bitcast.115), kind=kLoop, calls=%fused_computation.6 | loop fusion | flops 18873344 | bytes 8415232 | tf_op jit(solution)/shard_map/reduce_sum | solution.py:68
  145.1 3.9 fusion.45
  149.8 3.5 all-to-all-start.1
  153.4 24.8 %all-gather.5.cloned.1.call-done = bf16[1024,2048]{1,0:T(8,128)(2,1)} async-done(((bf16[1024,128]{1,0:T(8,128)(2,1)}), bf16[1024,2048]{1,0:T(8,128)(2,1)}) %all-gather.5.cloned.1.call-update) | async-done | bytes 4194320 | tf_op jit(solution)/shard_map/all_gather | solution.py:116
  178.2 3.9 fusion.89
  182.7 20.3 %reduce-scatter.3.cloned.1.call-done = f32[128,1024]{1,0:T(8,128)} async-done(((f32[128,2048]{1,0:T(8,128)}), f32[128,1024]{1,0:T(8,128)}) %reduce-scatter.3.cloned.1.call-update) | async-done | bytes 524304 | tf_op jit(solution)/shard_map/reduce_scatter | solution.py:147
  204.8 7.3 %all-reduce = (f32[128]{0:T(128)S(1)}, f32[128,64]{0,1:T(8,128)S(1)}) all-reduce(f32[128]{0:T(128)S(1)} %get-tuple-element.7, f32[128,64]{0,1:T(8,128)S(1)} %fusion.50), channel_id=1, replica_groups=mesh['dp'=16,'mp'=2] {'mp'}, use_global_device_ids=true, to_apply=%region_12.13 | all-reduce | flops 8320 | bytes 66560 | tf_op jit(solution)/shard_map/psum | solution.py:152
  212.3 7.0 %all_gather.15 = bf16[128,2048]{1,0:T(8,128)(2,1)S(1)} all-gather(bf16[128,1024]{1,0:T(8,128)(2,1)S(1)} %fusion.51), channel_id=1, replica_groups=mesh['dp'=16,'mp'=2] {'mp'}, dimensions={1}, use_global_device_ids=true | all-gather | bytes 786432 | tf_op jit(solution)/shard_map/all_gather | solution.py:183
  220.6 98.4 %all_to_all.20 = bf16[16,2,32,2048]{3,2,1,0:T(8,128)(2,1)S(1)} all-to-all(bf16[16,2,32,2048]{3,2,1,0:T(8,128)(2,1)S(1)} %bitcast.92), channel_id=1, replica_groups=mesh['dp'=16,'mp'=2] {'dp'}, dimensions={0} | all-to-all | bytes 8388608 | tf_op jit(solution)/shard_map/all_to_all | solution.py:185
  319.5 2.5 slice-done.1
  322.0 3.7 fusion.11
  325.6 3.7 fusion.7
  329.4 10.5 %fusion.21 = bf16[512,2048]{1,0:T(8,128)(2,1)} fusion(bf16[1,2048,2048]{2,1,0:T(8,128)(2,1)} %param.31, f32[512,1024]{1,0:T(8,128)} %fusion.11, bf16[512,2048]{1,0:T(8,128)(2,1)} %bitcast.99, bf16[2048,2048]{1,0:T(8,128)(2,1)} %bitcast.123), kind=kOutput, calls=%fused_computation.25 | convolution fusion | flops 4299161600 | bytes 14680064 | tf_op jit(solution)/shard_map/dot_general | solution.py:195
  339.9 10.0 %fusion.24 = bf16[512,2048]{1,0:T(8,128)(2,1)} fusion(bf16[1,2048,2048]{2,1,0:T(8,128)(2,1)} %param.31, f32[512,1024]{1,0:T(8,128)} %fusion.7, bf16[512,2048]{1,0:T(8,128)(2,1)S(1)} %bitcast.97, bf16[2048,2048]{1,0:T(8,128)(2,1)} %bitcast.124), kind=kOutput, calls=%fused_computation.26 | convolution fusion | flops 4299161600 | bytes 14680064 | tf_op jit(solution)/shard_map/dot_general | solution.py:195
  349.9 4.6 pad_maximum_fusion
  354.5 5.3 %all-to-all-start.3 = ((bf16[16,2,32,2048]{3,2,1,0:T(8,128)(2,1)}), bf16[16,2,32,2048]{3,2,1,0:T(8,128)(2,1)}, u32[]{:S(2)}, u32[]{:S(2)}) async-start(bf16[16,2,32,2048]{3,2,1,0:T(8,128)(2,1)} %pad_maximum_fusion), calls=%async_computation.4 | async-start | bytes 8388608 | tf_op jit(solution)/shard_map/all_to_all | solution.py:197
  359.9 77.5 %all-to-all-done.3 = bf16[16,2,32,2048]{3,2,1,0:T(8,128)(2,1)} async-done(((bf16[16,2,32,2048]{3,2,1,0:T(8,128)(2,1)}), bf16[16,2,32,2048]{3,2,1,0:T(8,128)(2,1)}, u32[]{:S(2)}, u32[]{:S(2)}) %all-to-all-start.3) | async-done | bytes 4194336 | tf_op jit(solution)/shard_map/all_to_all | solution.py:197
  437.5 3.0 convolution_bitcast_fusion
  440.4 3.9 fusion.27
  444.4 35.4 %reduce-scatter.5.cloned.1.call-done = f32[128,1024]{1,0:T(8,128)} async-done(((f32[128,2048]{1,0:T(8,128)}), f32[128,1024]{1,0:T(8,128)}) %reduce-scatter.5.cloned.1.call-update) | async-done | bytes 524304 | tf_op jit(solution)/shard_map/reduce_scatter | solution.py:208
  479.8 1.8 fusion.54
  (88 shorter events, 17.7 us)
Async XLA Ops:
  6.5 197.6 %copy-start = (f32[1024,64]{0,1:T(8,128)S(1)}, f32[1024,64]{0,1:T(8,128)}, u32[]{:S(2)}) copy-start(f32[1024,64]{0,1:T(8,128)} %param.28) | copy-start | bytes 786436
  6.5 114.2 %all-gather.3.cloned.1.call-start = ((), (), s32[]{:S(2)}) async-start(), calls=%async_computation.6 | async-start | bytes 8912896 | tf_op jit(solution)/shard_map/all_gather | solution.py:51
  22.1 8.8 %copy-start.14 = (s32[4]{0:T(128)S(1)}, s32[4]{0:T(128)}, u32[]{:S(2)}) copy-start(s32[4]{0:T(128)} %param.17) | copy-start | bytes 52
  22.1 9.3 %copy-start.10 = (s32[2048]{0:T(1024)S(1)}, s32[2048]{0:T(1024)}, u32[]{:S(2)}) copy-start(s32[2048]{0:T(1024)} %param.18) | copy-start | bytes 24580
  24.0 53.6 %all-to-all-start = ((bf16[16,128,384]{2,1,0:T(8,128)(2,1)}), bf16[16,128,384]{2,1,0:T(8,128)(2,1)}, u32[]{:S(2)}, u32[]{:S(2)}) async-start(bf16[16,128,384]{2,1,0:T(8,128)(2,1)} %bitcast.10), calls=%async_computation | async-start | bytes 3145728 | tf_op jit(solution)/shard_map/all_to_all | solution.py:107
  30.2 148.0 %all-gather.5.cloned.1.call-start = ((), (), s32[]{:S(2)}) async-start(), calls=%async_computation.7 | async-start | bytes 4456448 | tf_op jit(solution)/shard_map/all_gather | solution.py:116
  120.7 8.0 %copy-start.13 = (f32[128]{0:T(128)S(1)}, f32[128]{0:T(128)}, u32[]{:S(2)}) copy-start(f32[128]{0:T(128)} %param.23) | copy-start | bytes 1540
  127.1 1.7 copy-start.3
  128.8 5.4 %copy-start.12 = (f32[128]{0:T(128)S(1)}, f32[128]{0:T(128)}, u32[]{:S(2)}) copy-start(f32[128]{0:T(128)} %param.22) | copy-start | bytes 1540
  134.0 1.3 copy-start.2
  134.4 2.0 copy-start.4
  134.4 2.1 copy-start.7
  134.4 2.2 copy-start.8
  149.0 33.3 %copy-start.11 = (s32[128,8]{0,1:T(8,128)S(1)}, s32[128,8]{0,1:T(8,128)}, u32[]{:S(2)}) copy-start(s32[128,8]{0,1:T(8,128)} %param.19) | copy-start | bytes 12292
  149.0 54.0 %copy-start.6 = (bf16[128,1024]{1,0:T(8,128)(2,1)S(1)}, bf16[128,1024]{1,0:T(8,128)(2,1)}, u32[]{:S(2)}) copy-start(bf16[128,1024]{1,0:T(8,128)(2,1)} %param.16) | copy-start | bytes 786436
  149.8 54.3 %copy-start.9 = (f32[1024]{0:T(1024)S(1)}, f32[1024]{0:T(1024)}, u32[]{:S(2)}) copy-start(f32[1024]{0:T(1024)} %param.21) | copy-start | bytes 12292
  149.8 28.4 %all-to-all-start.1 = ((bf16[8,128,128]{1,2,0:T(8,128)(2,1)}), bf16[8,128,128]{1,2,0:T(8,128)(2,1)S(1)}, u32[]{:S(2)}, u32[]{:S(2)}) async-start(bf16[8,128,128]{1,2,0:T(8,128)(2,1)} %copy.45), calls=%async_computation.1 | async-start | bytes 524288 | tf_op jit(solution)/shard_map/all_to_all | solution.py:137
  153.4 49.6 %reduce-scatter.3.cloned.1.call-start = ((), (), s32[]{:S(2)}) async-start(), calls=%async_computation.8 | async-start | bytes 1572864 | tf_op jit(solution)/shard_map/reduce_scatter | solution.py:147
  220.6 98.9 %slice-start = ((s8[8388608]{0:T(1024)(128)(4,1)}), s8[4194304]{0:T(1024)(128)(4,1)S(1)}, s32[]{:S(2)}) async-start(s8[8388608]{0:T(1024)(128)(4,1)} %bitcast.119), calls=%async_computation.10 | async-start | bytes 8388608
  319.0 2.9 slice-start.1
  319.5 6.2 %copy-start.5 = (bf16[16,1,32,2048]{3,2,1,0:T(8,128)(2,1)}, bf16[16,1,32,2048]{3,2,1,0:T(8,128)(2,1)S(1)}, u32[]{:S(2)}) copy-start(bf16[16,1,32,2048]{3,2,1,0:T(8,128)(2,1)S(1)} %get-tuple-element.9) | copy-start | bytes 6291460
  354.5 83.0 %all-to-all-start.3 = ((bf16[16,2,32,2048]{3,2,1,0:T(8,128)(2,1)}), bf16[16,2,32,2048]{3,2,1,0:T(8,128)(2,1)}, u32[]{:S(2)}, u32[]{:S(2)}) async-start(bf16[16,2,32,2048]{3,2,1,0:T(8,128)(2,1)} %pad_maximum_fusion), calls=%async_computation.4 | async-start | bytes 8388608 | tf_op jit(solution)/shard_map/all_to_all | solution.py:197
  359.8 120.0 %reduce-scatter.5.cloned.1.call-start = ((), (), s32[]{:S(2)}) async-start(), calls=%async_computation.9 | async-start | bytes 1572864 | tf_op jit(solution)/shard_map/reduce_scatter | solution.py:208
  437.5 44.1 %copy-start.1 = (f32[1024,64]{0,1:T(8,128)S(1)}, f32[1024,64]{0,1:T(8,128)}, u32[]{:S(2)}) copy-start(f32[1024,64]{0,1:T(8,128)} %param.28) | copy-start | bytes 786436
Sparse Core Ops, SparseCore 0:
  18.9 101.8 all-gather.2
  122.9 55.2 all-gather.4
  182.2 20.6 reduce-scatter.2
  444.5 35.2 reduce-scatter.4

commit v2 on v1

--- a/solution.py
+++ b/solution.py
@@ -1,6 +1,8 @@
 import jax
 import jax.numpy as jnp
 from jax import lax
+from jax.experimental import pallas as pl
+from jax.experimental.pallas import tpu as pltpu
 from jax.sharding import PartitionSpec as P
 
 D = 2048
@@ -47,8 +49,154 @@
     return (segment, global_row - begin)
 
 
-def gather_tokens(block):
-    return lax.all_gather(block, "dp", axis=0, tiled=True)
+MESH = pl.DeviceIdType.MESH
+
+
+def gather_kernel(block_ref, out_ref, local_sem, a_sem, up_sem, down_sem, b_sem, twin_sem, recv_sem):
+    index = lax.axis_index("dp")
+    x = lax.axis_index("mp")
+    layers = lax.axis_size("dp") // 4
+    z, y, core = index // 4, (index // 2) % 2, index % 2
+    rows, width = block_ref.shape
+    to_a = (index + core * (2 - 4 * y), x + (1 - core) * (1 - 2 * x))
+    to_b = (index + (1 - core) * (2 - 4 * y), x + core * (1 - 2 * x))
+    to_twin = (index + 1 - 2 * core, x)
+    to_up, to_down = (index + 4, x), (index - 4, x)
+
+    def place(layer, da, db, which):
+        dy = which * da + (1 - which) * db
+        dx = (1 - which) * da + which * db
+        yy, xx = y + dy * (1 - 2 * y), x + dx * (1 - 2 * x)
+        return layer * 4 + yy * 2 + which, xx
+
+    def view(spot):
+        return out_ref.at[
+            pl.ds(pl.multiple_of(spot[0] * rows, rows), rows),
+            pl.ds(pl.multiple_of(spot[1] * width, width), width),
+        ]
+
+    def send(spot, sem, device, own=False):
+        return pltpu.make_async_remote_copy(
+            src_ref=block_ref if own else view(spot),
+            dst_ref=view(spot),
+            send_sem=sem,
+            recv_sem=recv_sem.at[spot[0] * 2 + spot[1]],
+            device_id=device,
+            device_id_type=MESH,
+        )
+
+    def arrive(spot):
+        send(spot, local_sem, to_twin).wait_recv()
+
+    barrier = pltpu.get_barrier_semaphore()
+    for peer in (to_a, to_b, to_twin):
+        pl.semaphore_signal(barrier, inc=1, device_id=peer, device_id_type=MESH)
+    has_up, has_down = z < layers - 1, z > 0
+
+    @pl.when(has_up)
+    def _():
+        pl.semaphore_signal(barrier, inc=1, device_id=to_up, device_id_type=MESH)
+
+    @pl.when(has_down)
+    def _():
+        pl.semaphore_signal(barrier, inc=1, device_id=to_down, device_id_type=MESH)
+
+    pl.semaphore_wait(
+        barrier, 3 + has_up.astype(jnp.int32) + has_down.astype(jnp.int32)
+    )
+
+    home = place(z, 0, 0, core)
+    keep = pltpu.make_async_copy(block_ref, view(home), local_sem)
+    first = send(home, a_sem, to_a, True)
+
+    def spread(layer, da, own, act):
+        spot = place(layer, da, 0, core)
+        slot = layer * 2 + da
+
+        @pl.when((layer <= z) & has_up)
+        def _():
+            act(send(spot, up_sem.at[slot], to_up, own))
+
+        @pl.when((layer >= z) & has_down)
+        def _():
+            act(send(spot, down_sem.at[slot], to_down, own))
+
+        act(send(spot, b_sem.at[slot], to_b, own))
+        act(send(spot, twin_sem.at[slot * 2], to_twin, own))
+
+    def hand_over(layer, da, act):
+        spot = place(layer, da, 1, core)
+        act(send(spot, twin_sem.at[(layer * 2 + da) * 2 + 1], to_twin))
+
+    start = lambda copy: copy.start()
+    finish = lambda copy: copy.wait_send()
+    first.start()
+    spread(z, 0, True, start)
+    keep.start()
+    arrive(place(z, 1, 0, core))
+    spread(z, 1, False, start)
+
+    def both(distance, run):
+        for da in range(2):
+            @pl.when(z >= distance)
+            def _():
+                run(z - distance, da)
+
+            @pl.when(z + distance < layers)
+            def _():
+                run(z + distance, da)
+
+    def onward(layer, da):
+        arrive(place(layer, da, 0, core))
+        spread(layer, da, False, start)
+
+    def across(layer, da):
+        arrive(place(layer, da, 1, core))
+        hand_over(layer, da, start)
+
+    for distance in range(1, layers):
+        both(distance, onward)
+        if distance == 1:
+            for da in range(2):
+                across(z, da)
+        else:
+            both(distance - 1, across)
+    both(layers - 1, across)
+    keep.wait()
+    first.wait_send()
+    for layer in range(layers):
+        for da in range(2):
+            spread(layer, da, False, finish)
+            hand_over(layer, da, finish)
+            for db in range(2):
+                arrive(place(layer, da, db, 1 - core))
+
+
+def gather_blocks(block):
+    dp_count, mp_count = lax.axis_size("dp"), lax.axis_size("mp")
+    rows, width = block.shape
+    if mp_count != 2 or dp_count % 4:
+        wide = lax.all_gather(block, "mp", axis=1, tiled=True)
+        return lax.all_gather(wide, "dp", axis=0, tiled=True)
+    layers = dp_count // 4
+    dma = pltpu.SemaphoreType.DMA
+    return pl.pallas_call(
+        gather_kernel,
+        out_shape=jax.ShapeDtypeStruct((dp_count * rows, mp_count * width), block.dtype),
+        in_specs=[pl.BlockSpec(memory_space=pl.ANY)],
+        out_specs=pl.BlockSpec(memory_space=pl.ANY),
+        scratch_shapes=[
+            dma,
+            dma,
+            dma((layers * 2,)),
+            dma((layers * 2,)),
+            dma((layers * 2,)),
+            dma((layers * 4,)),
+            dma((dp_count * mp_count,)),
+        ],
+        compiler_params=pltpu.CompilerParams(collective_id=0, has_side_effects=True),
+        name="gather_blocks",
+    )(block)
 
 
 def attention(queries, keys, values, query_seg, query_row, key_seg, key_row, keep_mask):
@@ -107,12 +255,14 @@
     head_weight = lax.all_to_all(packed, "dp", split_axis=0, concat_axis=0, tiled=True)
     head_weight = head_weight.reshape(dp_count * weight_rows, 3 * HEAD_DIM)
 
-    full_tokens = lax.all_gather(tokens, "mp", axis=1, tiled=True)
-    xfloat = full_tokens.astype(jnp.float32)
-    normed_in = (
+    all_tokens = gather_blocks(tokens)
+    xfloat = all_tokens.astype(jnp.float32)
+    all_in = (
         xfloat * lax.rsqrt(jnp.mean(xfloat * xfloat, axis=1, keepdims=True) + EPS) * attention_gain
     ).astype(jnp.bfloat16)
-    all_in = gather_tokens(normed_in)
+    all_routes = lax.all_gather(routes, "dp", axis=0, tiled=True)
+    all_gain = lax.all_gather(mixture_gain, "mp", axis=0, tiled=True)
+    all_router = lax.all_gather(router_weight, "mp", axis=0, tiled=True)
     all_output_weight = lax.all_gather(output_weight, "dp", axis=1, tiled=True)
 
     key_row = jnp.arange(total_rows, dtype=jnp.int32)
@@ -146,23 +296,30 @@
     partial_out = jnp.dot(attended, all_output_weight, preferred_element_type=jnp.float32)
     summed_out = lax.psum_scatter(partial_out, "mp", scatter_dimension=1, tiled=True)
     residual = (tokens.astype(jnp.float32) + summed_out).astype(jnp.bfloat16)
-    hfloat = residual.astype(jnp.float32)
-    scaled = hfloat * mixture_gain
-    partial_logits = jnp.dot(scaled, router_weight, precision=lax.Precision.HIGHEST)
-    square_sum, logit_sum = lax.psum((jnp.sum(hfloat * hfloat, axis=1), partial_logits), "mp")
-    inverse = lax.rsqrt(square_sum / D + EPS)[:, None]
-    mixed_in = (scaled * inverse).astype(jnp.bfloat16)
-    logits = logit_sum * inverse
-
-    experts = jnp.arange(EXPERTS, dtype=jnp.int32)
-    named = jnp.any(routes[None, :, :] == experts[:, None, None], axis=2)
-    named_float = named.astype(jnp.float32)
-    sigmoid_vals = jax.nn.sigmoid(logits).T * named_float
-    route_weight = sigmoid_vals / jnp.sum(sigmoid_vals, axis=0, keepdims=True)
+    all_residual = gather_blocks(residual)
+    hfloat = all_residual.astype(jnp.float32)
+    inverse = lax.rsqrt(jnp.mean(hfloat * hfloat, axis=1, keepdims=True) + EPS)
+    mixed_in = (hfloat * all_gain * inverse).astype(jnp.bfloat16)
+
+    own_rows = lax.dynamic_slice_in_dim(all_residual, dp_index * tok_rows, tok_rows, 0)
+    own_float = own_rows.astype(jnp.float32)
+    own_inverse = lax.rsqrt(jnp.mean(own_float * own_float, axis=1, keepdims=True) + EPS)
+    logits = (
+        jnp.dot(own_float * all_gain, all_router, precision=lax.Precision.HIGHEST) * own_inverse
+    )
+
     ids = jnp.arange(tok_rows, dtype=jnp.int32)
     earlier = (ids[:, None] < ids[None, :]).astype(jnp.bfloat16)
-    before = jnp.dot(named.astype(jnp.bfloat16), earlier, preferred_element_type=jnp.float32)
-    place = jnp.where(named, before.astype(jnp.int32), -1)
+    slots = jnp.arange(CAP, dtype=jnp.int32)
+
+    def chosen_slots(named):
+        before = jnp.dot(
+            named.astype(jnp.bfloat16).reshape(-1, tok_rows),
+            earlier,
+            preferred_element_type=jnp.float32,
+        ).reshape(named.shape)
+        place = jnp.where(named, before.astype(jnp.int32), -1)
+        return place[:, :, None, :] == slots[None, None, :, None]
 
     exp_local = EXPERTS // dp_count
     gate_local = expert_gate[0]
@@ -173,18 +330,17 @@
     units = unit_count // held
     first_expert = (mp_index * unit_count) // FF
 
-    def mine(table):
-        split = table.reshape(dp_count, exp_local, tok_rows)
-        return lax.dynamic_slice_in_dim(split, first_expert, held, 1)
-
-    slots = jnp.arange(CAP, dtype=jnp.int32)
-    chosen = mine(place)[:, :, None, :] == slots[None, None, :, None]
-    select = chosen.astype(jnp.bfloat16).reshape(dp_count * held * CAP, tok_rows)
-    full_in = lax.all_gather(mixed_in, "mp", axis=1, tiled=True)
-    sending = jnp.dot(select, full_in, preferred_element_type=jnp.float32).astype(jnp.bfloat16)
-    rows_in = lax.all_to_all(
-        sending.reshape(dp_count, held, CAP, D), "dp", split_axis=0, concat_axis=0, tiled=True
-    )
+    own_experts = dp_index * exp_local + first_expert + jnp.arange(held, dtype=jnp.int32)
+    block_routes = all_routes.reshape(dp_count, tok_rows, TOPK)
+    here = jnp.any(block_routes[:, None] == own_experts[None, :, None, None], axis=3)
+    select = chosen_slots(here).astype(jnp.bfloat16).reshape(dp_count, held * CAP, tok_rows)
+    rows_in = lax.dot_general(
+        select,
+        mixed_in.reshape(dp_count, tok_rows, D),
+        (((2,), (1,)), ((0,), (0,))),
+        preferred_element_type=jnp.float32,
+    ).astype(jnp.bfloat16)
+    rows_in = rows_in.reshape(dp_count, held, CAP, D)
     outs = []
     for index in range(held):
         rows = rows_in[:, index].reshape(dp_count * CAP, D)
@@ -197,7 +353,16 @@
     returned = lax.all_to_all(
         jnp.stack(outs, axis=1), "dp", split_axis=0, concat_axis=0, tiled=True
     ).reshape(dp_count * held * CAP, D)
-    spread = jnp.where(chosen, mine(route_weight)[:, :, None, :], 0.0)
+    experts = jnp.arange(EXPERTS, dtype=jnp.int32)
+    named = jnp.any(routes[None, :, :] == experts[:, None, None], axis=2)
+    sigmoid_vals = jax.nn.sigmoid(logits).T * named.astype(jnp.float32)
+    route_weight = sigmoid_vals / jnp.sum(sigmoid_vals, axis=0, keepdims=True)
+
+    def mine(table):
+        split = table.reshape(dp_count, exp_local, tok_rows)
+        return lax.dynamic_slice_in_dim(split, first_expert, held, 1)
+
+    spread = jnp.where(chosen_slots(mine(named)), mine(route_weight)[:, :, None, :], 0.0)
     spread = spread.reshape(dp_count * held * CAP, tok_rows)
     spread_high = spread.astype(jnp.bfloat16)
     spread_mid = (spread - spread_high.astype(jnp.float32)).astype(jnp.bfloat16)
@@ -206,7 +371,7 @@
         spread_high, returned, contract, preferred_element_type=jnp.float32
     ) + lax.dot_general(spread_mid, returned, contract, preferred_element_type=jnp.float32)
     mixture = lax.psum_scatter(mixture, "mp", scatter_dimension=1, tiled=True)
-    return (hfloat + mixture).astype(jnp.bfloat16)
+    return (residual.astype(jnp.float32) + mixture).astype(jnp.bfloat16)
 
 
 def solution(mesh):

time: 494 us -> 444 us (0.90)
  Pallas kernels: 0 us -> 144 us
  waiting for transfers between devices: 241 us -> 101 us
  blocking collectives: 123 us -> 45.2 us
  other arithmetic: 24.8 us -> 44.1 us
  matrix products: 54.4 us -> 63.3 us
    pallas_call x0 -> x2, Pallas kernels: none -> 144 us  [gather_blocks(): pl.pallas_call(gather_kernel, out_shape=jax.ShapeDtypeStruct((dp_count *...]
    all_to_all x1, blocking collectives: 98.4 us -> 12.1 us  [local(): lax.all_to_all(attended.reshape(local_heads, tok_rows, HEAD_DIM), 'dp', s...]
    all_gather x1 -> x0, waiting for transfers between devices: 43.2 us -> none  [gather_tokens(): return lax.all_gather(block, 'dp', axis=0, tiled=True)]
    all_to_all x1, waiting for transfers between devices: 39.4 us -> 0.01 us  [local(): lax.all_to_all(packed, 'dp', split_axis=0, concat_axis=0, tiled=True)]
    all_gather x1, waiting for transfers between devices: 24.8 us -> 0.01 us  [local(): all_output_weight = lax.all_gather(output_weight, 'dp', axis=1, tiled=True)]
    reduce_scatter x1, waiting for transfers between devices: 20.3 us -> 0.01 us  [local(): lax.psum_scatter(partial_out, 'mp', scatter_dimension=1, tiled=True)]
    all_gather x2 -> x3, blocking collectives: 17.3 us -> 33 us  [the longest x1 19.5 us: local(): all_routes = lax.all_gather(routes, 'dp', axis=0, tiled=True)]
    all_to_all x1, waiting for transfers between devices: 77.5 us -> 64.5 us  [local(): lax.all_to_all(jnp.stack(outs, axis=1), 'dp', split_axis=0, concat_axis=0...]
  transfers between devices with their start and end apart: 7 -> 5, of which waited for: 6 -> 2; matrix products, arithmetic and copies ran while one was open for 8% -> 10% of each run, Pallas kernels for 0% -> 23%
where the time goes in v2:
time: 444 us; the launch traced here: 437 us
  Pallas kernels  144 us (32%)
  waiting for transfers between devices  101 us (23%)
  matrix products  63.3 us (14%)
  blocking collectives  45.2 us (10%)
  other arithmetic  44.1 us (10%)
  local copies, waits for them, and re-layouts  13.9 us (3%)
  between operations  13.9 us (3%)
  starting transfers between devices  12.2 us (3%)
    pallas_call x2, Pallas kernels, gather_blocks(): pl.pallas_call(gather_kernel, out_shape=jax.ShapeDtypeStruct((dp_count *...  144 us
    all_to_all x1, waiting for transfers between devices, local(): lax.all_to_all(jnp.stack(outs, axis=1), 'dp', split_axis=0, concat_axis=0...  64.5 us
    reduce_scatter x1, waiting for transfers between devices, local(): mixture = lax.psum_scatter(mixture, 'mp', scatter_dimension=1, tiled=True)  35.4 us
    dot_general x2, matrix products, local(): jnp.dot(hidden, down_local[low:high], preferred_element_type=jnp.float32)  20.7 us
    all_gather x1, blocking collectives, local(): all_routes = lax.all_gather(routes, 'dp', axis=0, tiled=True)  19.5 us
    all_to_all x1, blocking collectives, local(): lax.all_to_all(attended.reshape(local_heads, tok_rows, HEAD_DIM), 'dp', s...  12.1 us
    dot_general x2, matrix products, local(): jnp.dot(rows, gate_local[:, low:high], preferred_element_type=jnp.float32)  10.6 us
    all_gather x1, blocking collectives, local(): all_router = lax.all_gather(router_weight, 'mp', axis=0, tiled=True)  9.16 us
  transfers between devices with their start and end apart: 5, of which 2 were waited for; matrix products, arithmetic and copies ran while one was open for 10% of the time, Pallas kernels for 23%

profile of v2, /device:TPU:0, one launch (start us, length us, event | category | flops | bytes accessed | tf_op | source)
XLA Modules:
  0.0 437.5 jit_solution(13092137172360934381)
XLA Ops:
  11.8 7.4 %all-to-all-start = ((bf16[16,128,384]{2,1,0:T(8,128)(2,1)}), bf16[16,128,384]{2,1,0:T(8,128)(2,1)}, u32[]{:S(2)}, u32[]{:S(2)}) async-start(bf16[16,128,384]{2,1,0:T(8,128)(2,1)} %bitcast.10), calls=%async_computation | async-start | bytes 3145728 | tf_op jit(solution)/shard_map/all_to_all | solution.py:255
  20.0 100.2 %gather_blocks.2 = bf16[2048,2048]{1,0:T(8,128)(2,1)} custom-call(bf16[128,1024]{1,0:T(8,128)(2,1)} %block_ref.1), custom_call_target="tpu_custom_call" | custom-call | tf_op jit(solution)/shard_map/gather_blocks/pallas_call | solution.py:183
  120.7 5.1 %fusion = f32[2048]{0:T(1024)S(1)} fusion(bf16[2048,2048]{1,0:T(8,128)(2,1)} %gather_blocks.2), kind=kLoop, calls=%fused_computation.4 | loop fusion | flops 12580864 | bytes 8396800 | tf_op jit(solution)/shard_map/reduce_sum | solution.py:261
  125.8 3.7 multiply_cosine_fusion
  129.5 3.1 multiply_sine_fusion.1
  132.6 6.7 %fusion.6 = f32[2048,384]{0,1:T(8,128)S(1)} fusion(bf16[2048,384]{1,0:T(8,128)(2,1)} %bitcast.11, bf16[2048,2048]{1,0:T(8,128)(2,1)} %gather_blocks.2, f32[2048]{0:T(1024)S(1)} %copy-done.14, f32[2048]{0:T(1024)S(1)} %add_rsqrt_fusion.2), kind=kOutput, calls=%fused_computation.10 | convolution fusion | flops 3238002688 | bytes 13123584 | tf_op jit(solution)/shard_map/dot_general | solution.py:277
  142.6 3.1 reshape.390
  150.4 3.4 fusion.12
  153.9 5.3 %fusion.13 = f32[1024]{0:T(1024)S(1)} fusion(f32[1024,2048]{1,0:T(8,128)S(1)} %get-tuple-element.20, f32[1024]{0:T(1024)S(1)} %get-tuple-element.19, s32[1024]{0:T(1024)S(1)} %bitcast.117, pred[2048]{0:T(1024)(128)(4,1)S(1)} %broadcast_compare_fusion, s32[2048]{0:T(1024)S(1)} %convert_reduce_fusion, s32[1024]{0:T(1024)S(1)} %bitcast.120), kind=kLoop, calls=%fused_computation.19 | loop fusion | flops 18873344 | bytes 8415232 | tf_op jit(solution)/shard_map/reduce_sum | solution.py:216
  159.2 3.9 fusion.60
  163.3 12.1 %all_to_all.15 = bf16[8,128,128]{1,2,0:T(8,128)(2,1)S(1)} all-to-all(bf16[8,128,128]{1,2,0:T(8,128)(2,1)S(1)} %copy.70), channel_id=1, replica_groups={{0,4,8,12,16,20,24,28},{2,6,10,14,18,22,26,30},{1,5,9,13,17,21,25,29},{..., dimensions={0} | all-to-all | bytes 524288 | tf_op jit(solution)/shard_map/all_to_all | solution.py:287
  175.4 3.9 fusion.105
  179.4 19.5 %all_gather.15 = s32[2048,8]{0,1:T(8,128)S(1)} all-gather(s32[128,8]{0,1:T(8,128)S(1)} %copy-done.9), channel_id=1, replica_groups=mesh['dp'=16,'mp'=2] {'dp'}, dimensions={0}, use_global_device_ids=true | all-gather | bytes 69632 | tf_op jit(solution)/shard_map/all_gather | solution.py:263
  199.5 4.3 all_gather.13
  203.8 1.8 add_convert_fusion.1.block_ref
  205.7 44.0 %gather_blocks.3 = bf16[2048,2048]{1,0:T(8,128)(2,1)} custom-call(bf16[128,1024]{1,0:T(8,128)(2,1)} %add_convert_fusion.1.block_ref), custom_call_target="tpu_custom_call" | custom-call | tf_op jit(solution)/shard_map/gather_blocks/pallas_call | solution.py:183
  249.7 5.1 %fusion.5 = f32[2048]{0:T(1024)S(1)} fusion(bf16[2048,2048]{1,0:T(8,128)(2,1)} %gather_blocks.3), kind=kLoop, calls=%fused_computation.9 | loop fusion | flops 12580864 | bytes 8396800 | tf_op jit(solution)/shard_map/reduce_sum | solution.py:301
  254.8 8.5 %fusion.4 = bf16[2048,2048]{1,0:T(8,128)(2,1)} fusion(bf16[2048,2048]{1,0:T(8,128)(2,1)} %gather_blocks.3, f32[2048]{0:T(1024)S(1)} %add_rsqrt_fusion, f32[2048]{0:T(1024)S(1)} %all_gather.13), kind=kLoop, calls=%fused_computation.8 | loop fusion | flops 16777216 | bytes 16793600 | tf_op jit(solution)/shard_map/convert_element_type | solution.py:302
  263.3 4.6 %convolution_convert_fusion = bf16[16,64,2048]{2,1,0:T(8,128)(2,1)S(1)} fusion(pred[16,64,128]{2,1,0:T(32,128)(4,1)S(1)} %bitcast_compare_fusion, bf16[16,128,2048]{2,1,0:T(8,128)(2,1)} %bitcast.94), kind=kOutput, calls=%fused_computation.37 | convolution fusion | flops 538968064 | bytes 12713984 | tf_op jit(solution)/shard_map/dot_general | solution.py:337
  268.4 6.8 %fusion.21 = f32[512,1024]{1,0:T(8,128)} fusion(bf16[512,2048]{1,0:T(8,128)(2,1)S(1)} %bitcast.101, bf16[2048,2048]{1,0:T(8,128)(2,1)} %bitcast.123), kind=kOutput, calls=%fused_computation.27 | convolution fusion | flops 2147483648 | bytes 8388608 | tf_op jit(solution)/shard_map/dot_general | solution.py:348
  275.2 3.8 fusion.17
  279.0 10.8 %fusion.31 = bf16[512,2048]{1,0:T(8,128)(2,1)} fusion(bf16[1,2048,2048]{2,1,0:T(8,128)(2,1)} %param.31, f32[512,1024]{1,0:T(8,128)} %fusion.21, bf16[512,2048]{1,0:T(8,128)(2,1)} %bitcast.102, bf16[2048,2048]{1,0:T(8,128)(2,1)} %bitcast.127), kind=kOutput, calls=%fused_computation.38 | convolution fusion | flops 4299161600 | bytes 14680064 | tf_op jit(solution)/shard_map/dot_general | solution.py:351
  289.8 9.9 %fusion.34 = bf16[512,2048]{1,0:T(8,128)(2,1)} fusion(bf16[1,2048,2048]{2,1,0:T(8,128)(2,1)} %param.31, f32[512,1024]{1,0:T(8,128)} %fusion.17, bf16[512,2048]{1,0:T(8,128)(2,1)S(1)} %bitcast.100, bf16[2048,2048]{1,0:T(8,128)(2,1)} %bitcast.128), kind=kOutput, calls=%fused_computation.39 | convolution fusion | flops 4299161600 | bytes 14680064 | tf_op jit(solution)/shard_map/dot_general | solution.py:351
  299.7 4.6 %pad_maximum_fusion = bf16[16,2,32,2048]{3,2,1,0:T(8,128)(2,1)} fusion(bf16[16,1,32,2048]{3,2,1,0:T(8,128)(2,1)} %bitcast.104, bf16[16,1,32,2048]{3,2,1,0:T(8,128)(2,1)} %bitcast.103), kind=kLoop, calls=%fused_computation.29 | loop fusion | flops 2097152 | bytes 8388608 | tf_op jit(solution)/shard_map/stack | solution.py:354
  304.3 4.7 %all-to-all-start.2 = ((bf16[16,2,32,2048]{3,2,1,0:T(8,128)(2,1)}), bf16[16,2,32,2048]{3,2,1,0:T(8,128)(2,1)}, u32[]{:S(2)}, u32[]{:S(2)}) async-start(bf16[16,2,32,2048]{3,2,1,0:T(8,128)(2,1)} %pad_maximum_fusion), calls=%async_computation.3 | async-start | bytes 8388608 | tf_op jit(solution)/shard_map/all_to_all | solution.py:353
  309.3 9.2 %all_gather.14 = f32[2048,64]{0,1:T(8,128)S(1)} all-gather(f32[1024,64]{0,1:T(8,128)S(1)} %copy-done.8), channel_id=1, replica_groups=mesh['dp'=16,'mp'=2] {'mp'}, dimensions={0}, use_global_device_ids=true | all-gather | bytes 786432 | tf_op jit(solution)/shard_map/all_gather | solution.py:265
  319.7 2.3 fusion.104
  322.1 64.5 %all-to-all-done.2 = bf16[16,2,32,2048]{3,2,1,0:T(8,128)(2,1)} async-done(((bf16[16,2,32,2048]{3,2,1,0:T(8,128)(2,1)}), bf16[16,2,32,2048]{3,2,1,0:T(8,128)(2,1)}, u32[]{:S(2)}, u32[]{:S(2)}) %all-to-all-start.2) | async-done | bytes 4194336 | tf_op jit(solution)/shard_map/all_to_all | solution.py:353
  386.6 2.9 convolution_bitcast_fusion
  389.5 4.0 fusion.37
  393.5 35.4 %reduce-scatter.5.cloned.1.call-done = f32[128,1024]{1,0:T(8,128)} async-done(((f32[128,2048]{1,0:T(8,128)}), f32[128,1024]{1,0:T(8,128)}) %reduce-scatter.5.cloned.1.call-update) | async-done | bytes 524304 | tf_op jit(solution)/shard_map/reduce_scatter | solution.py:373
  428.9 1.8 add_convert_fusion
  (93 shorter events, 17.0 us)
Async XLA Ops:
  11.8 120.9 %all-to-all-start = ((bf16[16,128,384]{2,1,0:T(8,128)(2,1)}), bf16[16,128,384]{2,1,0:T(8,128)(2,1)}, u32[]{:S(2)}, u32[]{:S(2)}) async-start(bf16[16,128,384]{2,1,0:T(8,128)(2,1)} %bitcast.10), calls=%async_computation | async-start | bytes 3145728 | tf_op jit(solution)/shard_map/all_to_all | solution.py:255
  19.2 156.3 %all-gather.2.cloned.1.call-start = ((), (), s32[]{:S(2)}) async-start(), calls=%async_computation.5 | async-start | bytes 4456448 | tf_op jit(solution)/shard_map/all_gather | solution.py:266
  19.9 183.9 %reduce-scatter.3.cloned.1.call-start = ((), (), s32[]{:S(2)}) async-start(), calls=%async_computation.6 | async-start | bytes 1572864 | tf_op jit(solution)/shard_map/reduce_scatter | solution.py:297
  20.0 100.2 %copy-start.15 = (s32[4]{0:T(128)S(1)}, s32[4]{0:T(128)}, u32[]{:S(2)}) copy-start(s32[4]{0:T(128)} %param.17) | copy-start | bytes 52
  20.0 100.6 %copy-start.10 = (s32[2048]{0:T(1024)S(1)}, s32[2048]{0:T(1024)}, u32[]{:S(2)}) copy-start(s32[2048]{0:T(1024)} %param.18) | copy-start | bytes 24580
  120.7 11.9 %copy-start.14 = (f32[2048]{0:T(1024)S(1)}, f32[2048]{0:T(1024)}, u32[]{:S(2)}) copy-start(f32[2048]{0:T(1024)} %param.20) | copy-start | bytes 24580
  132.6 8.3 %copy-start.13 = (f32[128]{0:T(128)S(1)}, f32[128]{0:T(128)}, u32[]{:S(2)}) copy-start(f32[128]{0:T(128)} %param.23) | copy-start | bytes 1540
  139.3 1.7 copy-start.1
  141.0 7.0 %copy-start.12 = (f32[128]{0:T(128)S(1)}, f32[128]{0:T(128)}, u32[]{:S(2)}) copy-start(f32[128]{0:T(128)} %param.22) | copy-start | bytes 1540
  147.8 1.3 copy-start
  148.2 2.0 copy-start.2
  148.2 2.1 copy-start.6
  148.2 2.2 copy-start.7
  163.1 16.3 %copy-start.9 = (s32[128,8]{0,1:T(8,128)S(1)}, s32[128,8]{0,1:T(8,128)}, u32[]{:S(2)}) copy-start(s32[128,8]{0,1:T(8,128)} %param.19) | copy-start | bytes 12292
  163.1 36.4 %copy-start.11 = (f32[1024]{0:T(1024)S(1)}, f32[1024]{0:T(1024)}, u32[]{:S(2)}) copy-start(f32[1024]{0:T(1024)} %param.21) | copy-start | bytes 12292
  163.1 40.8 %copy-start.5 = (bf16[128,1024]{1,0:T(8,128)(2,1)S(1)}, bf16[128,1024]{1,0:T(8,128)(2,1)}, u32[]{:S(2)}) copy-start(bf16[128,1024]{1,0:T(8,128)(2,1)} %block_ref.1) | copy-start | bytes 786436
  267.9 7.3 %slice-start = ((s8[8388608]{0:T(1024)(128)(4,1)}), s8[4194304]{0:T(1024)(128)(4,1)S(1)}, s32[]{:S(2)}) async-start(s8[8388608]{0:T(1024)(128)(4,1)} %bitcast.124), calls=%async_computation.8 | async-start | bytes 8388608
  268.3 6.8 %copy-start.4 = (bf16[16,1,32,2048]{3,2,1,0:T(8,128)(2,1)}, bf16[16,1,32,2048]{3,2,1,0:T(8,128)(2,1)S(1)}, u32[]{:S(2)}) copy-start(bf16[16,1,32,2048]{3,2,1,0:T(8,128)(2,1)S(1)} %get-tuple-element.5) | copy-start | bytes 6291460
  268.4 6.8 %slice-start.1 = ((s8[8388608]{0:T(1024)(128)(4,1)}), s8[4194304]{0:T(1024)(128)(4,1)S(1)}, s32[]{:S(2)}) async-start(s8[8388608]{0:T(1024)(128)(4,1)} %bitcast.124), calls=%async_computation.9 | async-start | bytes 8388608
  304.3 5.0 %copy-start.8 = (f32[1024,64]{0,1:T(8,128)S(1)}, f32[1024,64]{0,1:T(8,128)}, u32[]{:S(2)}) copy-start(f32[1024,64]{0,1:T(8,128)} %param.28) | copy-start | bytes 786436
  304.3 82.3 %all-to-all-start.2 = ((bf16[16,2,32,2048]{3,2,1,0:T(8,128)(2,1)}), bf16[16,2,32,2048]{3,2,1,0:T(8,128)(2,1)}, u32[]{:S(2)}, u32[]{:S(2)}) async-start(bf16[16,2,32,2048]{3,2,1,0:T(8,128)(2,1)} %pad_maximum_fusion), calls=%async_computation.3 | async-start | bytes 8388608 | tf_op jit(solution)/shard_map/all_to_all | solution.py:353
  309.0 119.9 %reduce-scatter.5.cloned.1.call-start = ((), (), s32[]{:S(2)}) async-start(), calls=%async_computation.7 | async-start | bytes 1572864 | tf_op jit(solution)/shard_map/reduce_scatter | solution.py:373
  389.5 39.4 %copy-start.3 = (bf16[128,1024]{1,0:T(8,128)(2,1)S(1)}, bf16[128,1024]{1,0:T(8,128)(2,1)}, u32[]{:S(2)}) copy-start(bf16[128,1024]{1,0:T(8,128)(2,1)} %add_convert_fusion.1.block_ref) | copy-start | bytes 786436
Sparse Core Ops, SparseCore 0:
  22.2 75.3 all-gather.1
  179.5 19.2 reduce-scatter.2
  393.7 35.2 reduce-scatter.4

commit v3 on v2

--- a/solution.py
+++ b/solution.py
@@ -197,6 +197,249 @@
         compiler_params=pltpu.CompilerParams(collective_id=0, has_side_effects=True),
         name="gather_blocks",
     )(block)
+
+
+def scatter_kernel(
+    parts_ref,
+    out_ref,
+    mine,
+    twin,
+    cross,
+    rise,
+    fall,
+    last,
+    total,
+    load_sem,
+    twin_send,
+    cross_send,
+    z_send,
+    last_send,
+    twin_recv,
+    cross_recv,
+    rise_recv,
+    fall_recv,
+    last_recv,
+):
+    index = lax.axis_index("dp")
+    x = lax.axis_index("mp")
+    layers = lax.axis_size("dp") // 4
+    z, y, core = index // 4, (index // 2) % 2, index % 2
+    rows, width = out_ref.shape
+    to_a = (index + core * (2 - 4 * y), x + (1 - core) * (1 - 2 * x))
+    to_b = (index + (1 - core) * (2 - 4 * y), x + core * (1 - 2 * x))
+    to_twin = (index + 1 - 2 * core, x)
+    to_up, to_down = (index + 4, x), (index - 4, x)
+    has_up, has_down = z < layers - 1, z > 0
+
+    def view(layer, da, db, which):
+        dy = which * da + (1 - which) * db
+        dx = (1 - which) * da + which * db
+        yy, xx = y + dy * (1 - 2 * y), x + dx * (1 - 2 * x)
+        row = (layer * 4 + yy * 2 + which) * rows
+        return parts_ref.at[
+            pl.ds(pl.multiple_of(row, rows), rows),
+            pl.ds(pl.multiple_of(xx * width, width), width),
+        ]
+
+    def remote(source, target, send_sem, recv_sem, device):
+        return pltpu.make_async_remote_copy(
+            src_ref=source,
+            dst_ref=target,
+            send_sem=send_sem,
+            recv_sem=recv_sem,
+            device_id=device,
+            device_id_type=MESH,
+        )
+
+    barrier = pltpu.get_barrier_semaphore()
+    for peer in (to_a, to_b, to_twin):
+        pl.semaphore_signal(barrier, inc=1, device_id=peer, device_id_type=MESH)
+
+    @pl.when(has_up)
+    def _():
+        pl.semaphore_signal(barrier, inc=1, device_id=to_up, device_id_type=MESH)
+
+    @pl.when(has_down)
+    def _():
+        pl.semaphore_signal(barrier, inc=1, device_id=to_down, device_id_type=MESH)
+
+    def outward(run):
+        for distance in range(layers - 1, 0, -1):
+            for da in range(2):
+                @pl.when(z + distance < layers)
+                def _():
+                    run(z + distance, da, True)
+
+                @pl.when(z >= distance)
+                def _():
+                    run(z - distance, da, False)
+
+    def home(run):
+        for da in (1, 0):
+            run(z, da, None)
+
+    def load(layer, da, db):
+        slot = (layer * 2 + da) * 2 + db
+        return pltpu.make_async_copy(view(layer, da, db, core), mine.at[slot], load_sem.at[slot])
+
+    def to_other_core(layer, da, db):
+        slot = (layer * 2 + da) * 2 + db
+        return remote(
+            view(layer, da, db, 1 - core),
+            twin.at[slot],
+            twin_send.at[slot],
+            twin_recv.at[slot],
+            to_twin,
+        )
+
+    def to_cross(layer, da):
+        pair = layer * 2 + da
+        return remote(
+            mine.at[pair * 2 + 1], cross.at[pair], cross_send.at[pair], cross_recv.at[pair], to_b
+        )
+
+    def upward(layer, da):
+        pair = layer * 2 + da
+        return remote(mine.at[pair * 2], rise.at[pair], z_send.at[pair], rise_recv.at[pair], to_up)
+
+    def downward(layer, da):
+        pair = layer * 2 + da
+        return remote(
+            mine.at[pair * 2], fall.at[pair], z_send.at[pair], fall_recv.at[pair], to_down
+        )
+
+    def to_last():
+        return remote(mine.at[(z * 2 + 1) * 2], last, last_send, last_recv, to_a)
+
+    def add(target, *sources):
+        step = 16
+
+        def body(turn, carry):
+            at = pl.ds(pl.multiple_of(turn * step, step), step)
+            value = sources[0][at, :].astype(jnp.float32)
+            for source in sources[1:]:
+                value = value + source[at, :].astype(jnp.float32)
+            target[at, :] = value.astype(target.dtype)
+            return carry
+
+        lax.fori_loop(0, rows // step, body, 0)
+
+    for db in (1, 0):
+        outward(lambda layer, da, up: load(layer, da, db).start())
+        home(lambda layer, da, up: load(layer, da, db).start())
+    pl.semaphore_wait(barrier, 3 + has_up.astype(jnp.int32) + has_down.astype(jnp.int32))
+    for db in (1, 0):
+        outward(lambda layer, da, up: to_other_core(layer, da, db).start())
+        home(lambda layer, da, up: to_other_core(layer, da, db).start())
+
+    def pair_up(layer, da, up):
+        slot = (layer * 2 + da) * 2 + 1
+        load(layer, da, 1).wait()
+        to_other_core(layer, da, 1).wait_recv()
+        add(mine.at[slot], mine.at[slot], twin.at[slot])
+        to_cross(layer, da).start()
+
+    outward(pair_up)
+    home(pair_up)
+
+    def collect(layer, da, target):
+        pair = layer * 2 + da
+        load(layer, da, 0).wait()
+        to_other_core(layer, da, 0).wait_recv()
+        to_cross(layer, da).wait_recv()
+        add(target, mine.at[pair * 2], twin.at[pair * 2], cross.at[pair])
+
+    def pass_on(layer, da, up):
+        pair = layer * 2 + da
+        collect(layer, da, total)
+        if up:
+            @pl.when(has_down)
+            def _():
+                upward(layer, da).wait_recv()
+                add(total, total, rise.at[pair])
+        else:
+            @pl.when(has_up)
+            def _():
+                downward(layer, da).wait_recv()
+                add(total, total, fall.at[pair])
+        add(mine.at[pair * 2], total)
+        (upward if up else downward)(layer, da).start()
+
+    outward(pass_on)
+
+    def settle(layer, da, up):
+        pair = layer * 2 + da
+        target = total if da else out_ref
+        collect(layer, da, target)
+
+        @pl.when(has_down)
+        def _():
+            upward(layer, da).wait_recv()
+            add(target, target, rise.at[pair])
+
+        @pl.when(has_up)
+        def _():
+            downward(layer, da).wait_recv()
+            add(target, target, fall.at[pair])
+
+        if da:
+            add(mine.at[pair * 2], total)
+            to_last().start()
+
+    home(settle)
+    to_last().wait_recv()
+    add(out_ref, out_ref, last)
+
+    def finish(layer, da, up):
+        to_other_core(layer, da, 0).wait_send()
+        to_other_core(layer, da, 1).wait_send()
+        to_cross(layer, da).wait_send()
+        if up is not None:
+            (upward if up else downward)(layer, da).wait_send()
+
+    outward(finish)
+    home(finish)
+    to_last().wait_send()
+
+
+def scatter_sum(parts):
+    dp_count, mp_count = lax.axis_size("dp"), lax.axis_size("mp")
+    rows, width = parts.shape[0] // dp_count, parts.shape[1] // mp_count
+    if mp_count != 2 or dp_count % 4:
+        halves = lax.psum_scatter(parts, "mp", scatter_dimension=1, tiled=True)
+        return lax.psum_scatter(halves, "dp", scatter_dimension=0, tiled=True)
+    pairs = dp_count // 2
+    dma = pltpu.SemaphoreType.DMA
+    block = (rows, width)
+    return pl.pallas_call(
+        scatter_kernel,
+        out_shape=jax.ShapeDtypeStruct(block, jnp.float32),
+        in_specs=[pl.BlockSpec(memory_space=pl.ANY)],
+        out_specs=pl.BlockSpec(memory_space=pltpu.VMEM),
+        scratch_shapes=[
+            pltpu.VMEM((2 * pairs,) + block, jnp.bfloat16),
+            pltpu.VMEM((2 * pairs,) + block, jnp.bfloat16),
+            pltpu.VMEM((pairs,) + block, jnp.bfloat16),
+            pltpu.VMEM((pairs,) + block, jnp.bfloat16),
+            pltpu.VMEM((pairs,) + block, jnp.bfloat16),
+            pltpu.VMEM(block, jnp.bfloat16),
+            pltpu.VMEM(block, jnp.float32),
+            dma((2 * pairs,)),
+            dma((2 * pairs,)),
+            dma((pairs,)),
+            dma((pairs,)),
+            dma,
+            dma((2 * pairs,)),
+            dma((pairs,)),
+            dma((pairs,)),
+            dma((pairs,)),
+            dma,
+        ],
+        compiler_params=pltpu.CompilerParams(
+            collective_id=1, has_side_effects=True, vmem_limit_bytes=40 * 1024 * 1024
+        ),
+        name="scatter_sum",
+    )(parts.astype(jnp.bfloat16))
 
 
 def attention(queries, keys, values, query_seg, query_row, key_seg, key_row, keep_mask):
@@ -255,7 +498,10 @@
     head_weight = lax.all_to_all(packed, "dp", split_axis=0, concat_axis=0, tiled=True)
     head_weight = head_weight.reshape(dp_count * weight_rows, 3 * HEAD_DIM)
 
-    all_tokens = gather_blocks(tokens)
+    all_tokens, head_weight, late_weight = lax.optimization_barrier(
+        (gather_blocks(tokens), head_weight, output_weight)
+    )
+    all_output_weight = lax.all_gather(late_weight, "dp", axis=1, tiled=True)
     xfloat = all_tokens.astype(jnp.float32)
     all_in = (
         xfloat * lax.rsqrt(jnp.mean(xfloat * xfloat, axis=1, keepdims=True) + EPS) * attention_gain
@@ -263,7 +509,6 @@
     all_routes = lax.all_gather(routes, "dp", axis=0, tiled=True)
     all_gain = lax.all_gather(mixture_gain, "mp", axis=0, tiled=True)
     all_router = lax.all_gather(router_weight, "mp", axis=0, tiled=True)
-    all_output_weight = lax.all_gather(output_weight, "dp", axis=1, tiled=True)
 
     key_row = jnp.arange(total_rows, dtype=jnp.int32)
     key_seg, key_pos = segment_info(lengths, key_row)
@@ -333,7 +578,8 @@
     own_experts = dp_index * exp_local + first_expert + jnp.arange(held, dtype=jnp.int32)
     block_routes = all_routes.reshape(dp_count, tok_rows, TOPK)
     here = jnp.any(block_routes[:, None] == own_experts[None, :, None, None], axis=3)
-    select = chosen_slots(here).astype(jnp.bfloat16).reshape(dp_count, held * CAP, tok_rows)
+    chosen = chosen_slots(here)
+    select = chosen.astype(jnp.bfloat16).reshape(dp_count, held * CAP, tok_rows)
     rows_in = lax.dot_general(
         select,
         mixed_in.reshape(dp_count, tok_rows, D),
@@ -341,6 +587,11 @@
         preferred_element_type=jnp.float32,
     ).astype(jnp.bfloat16)
     rows_in = rows_in.reshape(dp_count, held, CAP, D)
+    experts = jnp.arange(EXPERTS, dtype=jnp.int32)
+    named = jnp.any(routes[:, :, None] == experts[None, None, :], axis=1)
+    sigmoid_vals = jax.nn.sigmoid(logits) * named.astype(jnp.float32)
+    route_weight = sigmoid_vals / jnp.sum(sigmoid_vals, axis=1, keepdims=True)
+    all_weights = lax.all_gather(route_weight, "dp", axis=0, tiled=True)
     outs = []
     for index in range(held):
         rows = rows_in[:, index].reshape(dp_count * CAP, D)
@@ -350,27 +601,19 @@
         hidden = (jax.nn.silu(gate_val) * up_val).astype(jnp.bfloat16)
         out = jnp.dot(hidden, down_local[low:high], preferred_element_type=jnp.float32)
         outs.append(out.astype(jnp.bfloat16).reshape(dp_count, CAP, D))
-    returned = lax.all_to_all(
-        jnp.stack(outs, axis=1), "dp", split_axis=0, concat_axis=0, tiled=True
-    ).reshape(dp_count * held * CAP, D)
-    experts = jnp.arange(EXPERTS, dtype=jnp.int32)
-    named = jnp.any(routes[None, :, :] == experts[:, None, None], axis=2)
-    sigmoid_vals = jax.nn.sigmoid(logits).T * named.astype(jnp.float32)
-    route_weight = sigmoid_vals / jnp.sum(sigmoid_vals, axis=0, keepdims=True)
-
-    def mine(table):
-        split = table.reshape(dp_count, exp_local, tok_rows)
-        return lax.dynamic_slice_in_dim(split, first_expert, held, 1)
-
-    spread = jnp.where(chosen_slots(mine(named)), mine(route_weight)[:, :, None, :], 0.0)
-    spread = spread.reshape(dp_count * held * CAP, tok_rows)
+    first_own = dp_index * exp_local + first_expert
+    own_weights = lax.dynamic_slice_in_dim(all_weights, first_own, held, 1)
+    own_weights = own_weights.reshape(dp_count, tok_rows, held).transpose(0, 2, 1)
+    spread = jnp.where(chosen, own_weights[:, :, None, :], 0.0)
     spread_high = spread.astype(jnp.bfloat16)
-    spread_mid = (spread - spread_high.astype(jnp.float32)).astype(jnp.bfloat16)
-    contract = (((0,), (0,)), ((), ()))
-    mixture = lax.dot_general(
-        spread_high, returned, contract, preferred_element_type=jnp.float32
-    ) + lax.dot_general(spread_mid, returned, contract, preferred_element_type=jnp.float32)
-    mixture = lax.psum_scatter(mixture, "mp", scatter_dimension=1, tiled=True)
+    spread_low = (spread - spread_high.astype(jnp.float32)).astype(jnp.bfloat16)
+    contract = (((1,), (1,)), ((0,), (0,)))
+    both = jnp.concatenate([spread_high, spread_low], 2).reshape(
+        dp_count, held * 2 * CAP, tok_rows
+    )
+    out_rows = jnp.concatenate(sum([[out, out] for out in outs], []), axis=1)
+    parts = lax.dot_general(both, out_rows, contract, preferred_element_type=jnp.float32)
+    mixture = scatter_sum(parts.reshape(total_rows, D))
     return (residual.astype(jnp.float32) + mixture).astype(jnp.bfloat16)
 
 

time: 444 us -> 376 us (0.85)
  waiting for transfers between devices: 101 us -> 2.71 us
  blocking collectives: 45.2 us -> 69.2 us
  Pallas kernels: 144 us -> 164 us
  other arithmetic: 44.1 us -> 39 us
  starting transfers between devices: 12.2 us -> 7.69 us
    all_to_all x1 -> x0, waiting for transfers between devices: 64.5 us -> none  [local(): lax.all_to_all(jnp.stack(outs, axis=1), 'dp', split_axis=0, concat_axis=0...]
    pallas_call x0 -> x1, Pallas kernels: none -> 46.6 us  [scatter_sum(): pl.pallas_call(scatter_kernel, out_shape=jax.ShapeDtypeStruct(block, jnp....]
    reduce_scatter x1 -> x0, waiting for transfers between devices: 35.4 us -> none  [local(): mixture = lax.psum_scatter(mixture, 'mp', scatter_dimension=1, tiled=True)]
    pallas_call x2, Pallas kernels: 144 us -> 118 us  [gather_blocks(): pl.pallas_call(gather_kernel, out_shape=jax.ShapeDtypeStruct((dp_count *...]
    all_gather x0 -> x1, blocking collectives: none -> 20.3 us  [local(): all_weights = lax.all_gather(route_weight, 'dp', axis=0, tiled=True)]
    all_to_all x1, blocking collectives: 12.1 us -> 17.5 us  [local(): lax.all_to_all(attended.reshape(local_heads, tok_rows, HEAD_DIM), 'dp', s...]
    all_to_all x1 -> x0, starting transfers between devices: 4.68 us -> none  [local(): lax.all_to_all(jnp.stack(outs, axis=1), 'dp', split_axis=0, concat_axis=0...]
    another operation x2 -> x1, other arithmetic: 4.76 us -> 0.18 us  [the longest x1 4.58 us: local(): jnp.stack(outs, axis=1)]
  transfers between devices with their start and end apart: 5 -> 3, of which waited for: 2 -> 1; matrix products, arithmetic and copies ran while one was open for 10% -> 10% of each run, Pallas kernels for 23% -> 20%
where the time goes in v3:
time: 376 us; the launch traced here: 369 us
  Pallas kernels  164 us (44%)
  blocking collectives  69.2 us (18%)
  matrix products  59.5 us (16%)
  other arithmetic  39 us (10%)
  between operations  14.2 us (4%)
  local copies, waits for them, and re-layouts  12.9 us (3%)
  starting transfers between devices  7.69 us (2%)
    pallas_call x2, Pallas kernels, gather_blocks(): pl.pallas_call(gather_kernel, out_shape=jax.ShapeDtypeStruct((dp_count *...  118 us
    pallas_call x1, Pallas kernels, scatter_sum(): pl.pallas_call(scatter_kernel, out_shape=jax.ShapeDtypeStruct(block, jnp....  46.6 us
    dot_general x2, matrix products, local(): jnp.dot(hidden, down_local[low:high], preferred_element_type=jnp.float32)  20.7 us
    all_gather x1, blocking collectives, local(): all_weights = lax.all_gather(route_weight, 'dp', axis=0, tiled=True)  20.3 us
    all_gather x1, blocking collectives, local(): all_routes = lax.all_gather(routes, 'dp', axis=0, tiled=True)  19 us
    all_to_all x1, blocking collectives, local(): lax.all_to_all(attended.reshape(local_heads, tok_rows, HEAD_DIM), 'dp', s...  17.5 us
    dot_general x2, matrix products, local(): jnp.dot(rows, gate_local[:, low:high], preferred_element_type=jnp.float32)  10.5 us
    convert_element_type x1, other arithmetic, local(): mixed_in = (hfloat * all_gain * inverse).astype(jnp.bfloat16)  8.53 us
  transfers between devices with their start and end apart: 3, of which 1 were waited for; matrix products, arithmetic and copies ran while one was open for 10% of the time, Pallas kernels for 20%

profile of v3, /device:TPU:0, one launch (start us, length us, event | category | flops | bytes accessed | tf_op | source)
XLA Modules:
  0.0 369.4 jit_solution(15177092054301739530)
XLA Ops:
  10.4 1.5 broadcast_in_dim.32
  11.9 7.4 %all-to-all-start = ((bf16[16,128,384]{2,1,0:T(8,128)(2,1)}), bf16[16,128,384]{2,1,0:T(8,128)(2,1)S(1)}, u32[]{:S(2)}, u32[]{:S(2)}) async-start(bf16[16,128,384]{2,1,0:T(8,128)(2,1)} %bitcast.10), calls=%async_computation | async-start | bytes 3145728 | tf_op jit(solution)/shard_map/all_to_all | solution.py:498
  19.8 75.4 %gather_blocks.2 = bf16[2048,2048]{1,0:T(8,128)(2,1)} custom-call(bf16[128,1024]{1,0:T(8,128)(2,1)} %block_ref.1), custom_call_target="tpu_custom_call" | custom-call | tf_op jit(solution)/shard_map/gather_blocks/pallas_call | solution.py:183
  95.2 2.9 multiply_sine_fusion.1
  99.3 3.7 multiply_cosine_fusion
  103.0 5.3 %fusion = f32[2048]{0:T(1024)S(1)} fusion(bf16[2048,2048]{1,0:T(8,128)(2,1)} %gather_blocks.2), kind=kLoop, calls=%fused_computation.4 | loop fusion | flops 12580864 | bytes 8396800 | tf_op jit(solution)/shard_map/reduce_sum | solution.py:507
  108.3 4.1 %fusion.6 = f32[2048,384]{0,1:T(8,128)S(1)} fusion(bf16[2048,384]{1,0:T(8,128)(2,1)S(1)} %bitcast.94, bf16[2048,2048]{1,0:T(8,128)(2,1)S(1)} %copy-done, f32[2048]{0:T(1024)S(1)} %copy-done.16, f32[2048]{0:T(1024)S(1)} %add_rsqrt_fusion.2), kind=kOutput, calls=%fused_computation.10 | convolution fusion | flops 3238002688 | bytes 13123584 | tf_op jit(solution)/shard_map/dot_general | solution.py:522
  112.5 1.5 copy-done.1
  115.3 1.9 reshape.376
  117.2 1.7 constant_dynamic-slice_fusion
  122.4 3.4 fusion.20
  125.8 4.8 %fusion.24 = f32[1024]{0:T(1024)S(1)} fusion(f32[1024,2048]{1,0:T(8,128)S(1)} %get-tuple-element.26, f32[1024]{0:T(1024)S(1)} %get-tuple-element.25, s32[1024]{0:T(1024)S(1)} %bitcast.107, pred[2048]{0:T(1024)(128)(4,1)S(1)} %broadcast_compare_fusion, s32[2048]{0:T(1024)S(1)} %convert_reduce_fusion, s32[1024]{0:T(1024)S(1)} %bitcast.110), kind=kLoop, calls=%fused_computation.28 | loop fusion | flops 18873344 | bytes 8415232 | tf_op jit(solution)/shard_map/reduce_sum | solution.py:459
  130.6 3.9 %fusion.68 = bf16[1024,128]{1,0:T(8,128)(2,1)S(1)} fusion(f32[1024,2048]{1,0:T(8,128)S(1)} %get-tuple-element.26, f32[1024]{0:T(1024)S(1)} %get-tuple-element.25, f32[2048,384]{0,1:T(8,128)S(1)} %copy-done.2, f32[1024]{0:T(1024)S(1)} %fusion.24, s32[1024]{0:T(1024)S(1)} %bitcast.108, s32[2048]{0:T(1024)S(1)} %convert_reduce_fusion, s32[1024]{0:T(1024)S(1)} %bitcast.111, ...), kind=kOutput, calls=%fused_computation.75 | convolution fusion | flops 556007424 | bytes 9201664 | tf_op jit(solution)/shard_map/dot_general | solution.py:460
  134.7 17.5 %all_to_all.10 = bf16[8,128,128]{1,2,0:T(8,128)(2,1)S(1)} all-to-all(bf16[8,128,128]{1,2,0:T(8,128)(2,1)S(1)} %copy.62), channel_id=1, replica_groups={{0,4,8,12,16,20,24,28},{2,6,10,14,18,22,26,30},{1,5,9,13,17,21,25,29},{..., dimensions={0} | all-to-all | bytes 524288 | tf_op jit(solution)/shard_map/all_to_all | solution.py:532
  152.2 2.7 all-gather.2.cloned.1.call-done
  154.8 3.9 %fusion.103 = f32[128,2048]{1,0:T(8,128)} fusion(bf16[128,1024]{0,1:T(8,128)(2,1)S(1)} %bitcast.98, bf16[1024,2048]{1,0:T(8,128)(2,1)} %all-gather.2.cloned.1.call-done), kind=kOutput, calls=%fused_computation.145 | convolution fusion | flops 536870912 | bytes 5505024 | tf_op jit(solution)/shard_map/dot_general | solution.py:541
  158.8 19.0 %all_gather.16 = s32[2048,8]{0,1:T(8,128)S(1)} all-gather(s32[128,8]{0,1:T(8,128)S(1)} %copy-done.11), channel_id=1, replica_groups=mesh['dp'=16,'mp'=2] {'dp'}, dimensions={0}, use_global_device_ids=true | all-gather | bytes 69632 | tf_op jit(solution)/shard_map/all_gather | solution.py:509
  178.3 4.3 %all_gather.17 = f32[2048]{0:T(1024)S(1)} all-gather(f32[1024]{0:T(1024)S(1)} %copy-done.13), channel_id=1, replica_groups=mesh['dp'=16,'mp'=2] {'mp'}, dimensions={0}, use_global_device_ids=true | all-gather | bytes 12288 | tf_op jit(solution)/shard_map/all_gather | solution.py:510
  182.7 8.1 %all_gather.18 = f32[2048,64]{0,1:T(8,128)S(1)} all-gather(f32[1024,64]{0,1:T(8,128)S(1)} %copy-done.10), channel_id=1, replica_groups=mesh['dp'=16,'mp'=2] {'mp'}, dimensions={0}, use_global_device_ids=true | all-gather | bytes 786432 | tf_op jit(solution)/shard_map/all_gather | solution.py:511
  190.8 1.8 add_convert_fusion.1.block_ref
  192.6 42.2 %gather_blocks.3 = bf16[2048,2048]{1,0:T(8,128)(2,1)} custom-call(bf16[128,1024]{1,0:T(8,128)(2,1)} %add_convert_fusion.1.block_ref), custom_call_target="tpu_custom_call" | custom-call | tf_op jit(solution)/shard_map/gather_blocks/pallas_call | solution.py:183
  236.1 2.3 fusion.102
  238.4 20.3 %all_gather.19 = f32[2048,64]{0,1:T(8,128)S(1)} all-gather(f32[128,64]{0,1:T(8,128)S(1)} %broadcast_divide_fusion), channel_id=1, replica_groups=mesh['dp'=16,'mp'=2] {'dp'}, dimensions={0}, use_global_device_ids=true | all-gather | bytes 557056 | tf_op jit(solution)/shard_map/all_gather | solution.py:594
  258.9 5.1 %fusion.5 = f32[2048]{0:T(1024)S(1)} fusion(bf16[2048,2048]{1,0:T(8,128)(2,1)} %gather_blocks.3), kind=kLoop, calls=%fused_computation.9 | loop fusion | flops 12580864 | bytes 8396800 | tf_op jit(solution)/shard_map/reduce_sum | solution.py:546
  264.0 8.5 %fusion.4 = bf16[2048,2048]{1,0:T(8,128)(2,1)} fusion(bf16[2048,2048]{1,0:T(8,128)(2,1)} %gather_blocks.3, f32[2048]{0:T(1024)S(1)} %add_rsqrt_fusion, f32[2048]{0:T(1024)S(1)} %all_gather.17), kind=kLoop, calls=%fused_computation.8 | loop fusion | flops 16777216 | bytes 16793600 | tf_op jit(solution)/shard_map/convert_element_type | solution.py:547
  272.6 4.6 %convolution_convert_fusion = bf16[16,64,2048]{2,1,0:T(8,128)(2,1)S(1)} fusion(pred[16,64,128]{2,1,0:T(32,128)(4,1)S(1)} %bitcast_compare_fusion, bf16[16,128,2048]{2,1,0:T(8,128)(2,1)} %bitcast.85), kind=kOutput, calls=%fused_computation.45 | convolution fusion | flops 538968064 | bytes 12713984 | tf_op jit(solution)/shard_map/dot_general | solution.py:583
  277.6 6.9 %fusion.28 = f32[512,1024]{1,0:T(8,128)} fusion(bf16[512,2048]{1,0:T(8,128)(2,1)S(1)} %bitcast.92, bf16[2048,2048]{1,0:T(8,128)(2,1)} %bitcast.113), kind=kOutput, calls=%fused_computation.32 | convolution fusion | flops 2147483648 | bytes 8388608 | tf_op jit(solution)/shard_map/dot_general | solution.py:599
  284.5 3.7 fusion.32
  288.2 10.8 %fusion.45 = bf16[512,2048]{1,0:T(8,128)(2,1)} fusion(bf16[1,2048,2048]{2,1,0:T(8,128)(2,1)} %param.31, f32[512,1024]{1,0:T(8,128)} %fusion.28, bf16[512,2048]{1,0:T(8,128)(2,1)} %bitcast.93, bf16[2048,2048]{1,0:T(8,128)(2,1)} %bitcast.117), kind=kOutput, calls=%fused_computation.47 | convolution fusion | flops 4299161600 | bytes 14680064 | tf_op jit(solution)/shard_map/dot_general | solution.py:602
  299.0 9.9 %fusion.42 = bf16[512,2048]{1,0:T(8,128)(2,1)} fusion(bf16[1,2048,2048]{2,1,0:T(8,128)(2,1)} %param.31, f32[512,1024]{1,0:T(8,128)} %fusion.32, bf16[512,2048]{1,0:T(8,128)(2,1)S(1)} %bitcast.91, bf16[2048,2048]{1,0:T(8,128)(2,1)} %bitcast.118), kind=kOutput, calls=%fused_computation.46 | convolution fusion | flops 4299161600 | bytes 14680064 | tf_op jit(solution)/shard_map/dot_general | solution.py:602
  309.0 5.9 %fusion.21 = bf16[16,128,2048]{2,1,0:T(8,128)(2,1)S(1)} fusion(bf16[16,128,128]{2,1,0:T(8,128)(2,1)S(1)} %bitcast.99, bf16[16,32,2048]{2,1,0:T(8,128)(2,1)} %bitcast.120, bf16[16,32,2048]{2,1,0:T(8,128)(2,1)} %bitcast.121), kind=kOutput, calls=%fused_computation.27 | convolution fusion | flops 1111490560 | bytes 13107200 | tf_op jit(solution)/shard_map/dot_general | solution.py:615
  314.9 46.6 %scatter_sum.1 = f32[128,1024]{1,0:T(8,128)S(1)} custom-call(bf16[2048,2048]{1,0:T(8,128)(2,1)S(1)} %bitcast.84), custom_call_target="tpu_custom_call" | custom-call | tf_op jit(solution)/shard_map/scatter_sum/pallas_call | solution.py:414
  (94 shorter events, 13.7 us)
Async XLA Ops:
  6.5 12.8 %copy-start.17 = (s32[4]{0:T(128)S(1)}, s32[4]{0:T(128)}, u32[]{:S(2)}) copy-start(s32[4]{0:T(128)} %param.17) | copy-start | bytes 52
  9.9 85.2 %copy-start.12 = (s32[2048]{0:T(1024)S(1)}, s32[2048]{0:T(1024)}, u32[]{:S(2)}) copy-start(s32[2048]{0:T(1024)} %param.18) | copy-start | bytes 24580
  11.9 86.2 %all-to-all-start = ((bf16[16,128,384]{2,1,0:T(8,128)(2,1)}), bf16[16,128,384]{2,1,0:T(8,128)(2,1)S(1)}, u32[]{:S(2)}, u32[]{:S(2)}) async-start(bf16[16,128,384]{2,1,0:T(8,128)(2,1)} %bitcast.10), calls=%async_computation | async-start | bytes 3145728 | tf_op jit(solution)/shard_map/all_to_all | solution.py:498
  19.3 135.6 %all-gather.2.cloned.1.call-start = ((), (), s32[]{:S(2)}) async-start(), calls=%async_computation.3 | async-start | bytes 4456448 | tf_op jit(solution)/shard_map/all_gather | solution.py:504
  19.8 88.5 %copy-start.16 = (f32[2048]{0:T(1024)S(1)}, f32[2048]{0:T(1024)}, u32[]{:S(2)}) copy-start(f32[2048]{0:T(1024)} %param.20) | copy-start | bytes 24580
  98.1 1.2 copy-start.5
  98.1 92.7 %reduce-scatter.2.cloned.1.call-start = ((), (), s32[]{:S(2)}) async-start(), calls=%async_computation.4 | async-start | bytes 1572864 | tf_op jit(solution)/shard_map/reduce_scatter | solution.py:542
  98.4 9.9 %copy-start = (bf16[2048,2048]{1,0:T(8,128)(2,1)S(1)}, bf16[2048,2048]{1,0:T(8,128)(2,1)}, u32[]{:S(2)}) copy-start(bf16[2048,2048]{1,0:T(8,128)(2,1)} %gather_blocks.2) | copy-start | bytes 25165828
  99.3 9.0 %copy-start.6 = (bf16[16,128,384]{2,1,0:T(8,128)(2,1)S(1)}, bf16[16,128,384]{2,1,0:T(8,128)(2,1)}, u32[]{:S(2)}) copy-start(bf16[16,128,384]{2,1,0:T(8,128)(2,1)} %copy-done.5) | copy-start | bytes 4718596
  108.3 5.7 %copy-start.15 = (f32[128]{0:T(128)S(1)}, f32[128]{0:T(128)}, u32[]{:S(2)}) copy-start(f32[128]{0:T(128)} %param.23) | copy-start | bytes 1540
  112.4 1.7 copy-start.1
  112.4 7.6 %copy-start.14 = (f32[128]{0:T(128)S(1)}, f32[128]{0:T(128)}, u32[]{:S(2)}) copy-start(f32[128]{0:T(128)} %param.22) | copy-start | bytes 1540
  119.7 2.6 copy-start.2
  119.7 2.6 copy-start.8
  119.8 2.6 copy-start.9
  130.6 28.2 %copy-start.11 = (s32[128,8]{0,1:T(8,128)S(1)}, s32[128,8]{0,1:T(8,128)}, u32[]{:S(2)}) copy-start(s32[128,8]{0,1:T(8,128)} %param.19) | copy-start | bytes 12292
  130.6 47.7 %copy-start.13 = (f32[1024]{0:T(1024)S(1)}, f32[1024]{0:T(1024)}, u32[]{:S(2)}) copy-start(f32[1024]{0:T(1024)} %param.21) | copy-start | bytes 12292
  130.6 52.1 %copy-start.10 = (f32[1024,64]{0,1:T(8,128)S(1)}, f32[1024,64]{0,1:T(8,128)}, u32[]{:S(2)}) copy-start(f32[1024,64]{0,1:T(8,128)} %param.28) | copy-start | bytes 786436
  134.5 56.3 %copy-start.7 = (bf16[128,1024]{1,0:T(8,128)(2,1)S(1)}, bf16[128,1024]{1,0:T(8,128)(2,1)}, u32[]{:S(2)}) copy-start(bf16[128,1024]{1,0:T(8,128)(2,1)} %block_ref.1) | copy-start | bytes 786436
  277.2 7.3 %slice-start = ((s8[8388608]{0:T(1024)(128)(4,1)}), s8[4194304]{0:T(1024)(128)(4,1)S(1)}, s32[]{:S(2)}) async-start(s8[8388608]{0:T(1024)(128)(4,1)} %bitcast.114), calls=%async_computation.5 | async-start | bytes 8388608
  277.6 10.6 %copy-start.4 = (bf16[16,1,32,2048]{3,2,1,0:T(8,128)(2,1)}, bf16[16,1,32,2048]{3,2,1,0:T(8,128)(2,1)S(1)}, u32[]{:S(2)}) copy-start(bf16[16,1,32,2048]{3,2,1,0:T(8,128)(2,1)S(1)} %get-tuple-element.12) | copy-start | bytes 6291460
  277.6 6.9 %slice-start.1 = ((s8[8388608]{0:T(1024)(128)(4,1)}), s8[4194304]{0:T(1024)(128)(4,1)S(1)}, s32[]{:S(2)}) async-start(s8[8388608]{0:T(1024)(128)(4,1)} %bitcast.114), calls=%async_computation.6 | async-start | bytes 8388608
  314.9 46.6 %copy-start.3 = (bf16[128,1024]{1,0:T(8,128)(2,1)S(1)}, bf16[128,1024]{1,0:T(8,128)(2,1)}, u32[]{:S(2)}) copy-start(bf16[128,1024]{1,0:T(8,128)(2,1)} %add_convert_fusion.1.block_ref) | copy-start | bytes 786436
Sparse Core Ops, SparseCore 0:
  98.2 56.5 all-gather.1
  158.9 18.7 reduce-scatter.1

commit v4 on v3

--- a/solution.py
+++ b/solution.py
@@ -507,8 +507,9 @@
         xfloat * lax.rsqrt(jnp.mean(xfloat * xfloat, axis=1, keepdims=True) + EPS) * attention_gain
     ).astype(jnp.bfloat16)
     all_routes = lax.all_gather(routes, "dp", axis=0, tiled=True)
-    all_gain = lax.all_gather(mixture_gain, "mp", axis=0, tiled=True)
-    all_router = lax.all_gather(router_weight, "mp", axis=0, tiled=True)
+    router_and_gain = jnp.concatenate([router_weight, mixture_gain[:, None]], axis=1)
+    router_and_gain = lax.all_gather(router_and_gain, "mp", axis=0, tiled=True)
+    all_router, all_gain = router_and_gain[:, :EXPERTS], router_and_gain[:, EXPERTS]
 
     key_row = jnp.arange(total_rows, dtype=jnp.int32)
     key_seg, key_pos = segment_info(lengths, key_row)
@@ -544,14 +545,9 @@
     all_residual = gather_blocks(residual)
     hfloat = all_residual.astype(jnp.float32)
     inverse = lax.rsqrt(jnp.mean(hfloat * hfloat, axis=1, keepdims=True) + EPS)
-    mixed_in = (hfloat * all_gain * inverse).astype(jnp.bfloat16)
-
-    own_rows = lax.dynamic_slice_in_dim(all_residual, dp_index * tok_rows, tok_rows, 0)
-    own_float = own_rows.astype(jnp.float32)
-    own_inverse = lax.rsqrt(jnp.mean(own_float * own_float, axis=1, keepdims=True) + EPS)
-    logits = (
-        jnp.dot(own_float * all_gain, all_router, precision=lax.Precision.HIGHEST) * own_inverse
-    )
+    scaled = hfloat * all_gain
+    mixed_in = (scaled * inverse).astype(jnp.bfloat16)
+    logits = jnp.dot(scaled, all_router, precision=lax.Precision.HIGHEST) * inverse
 
     ids = jnp.arange(tok_rows, dtype=jnp.int32)
     earlier = (ids[:, None] < ids[None, :]).astype(jnp.bfloat16)
@@ -588,10 +584,9 @@
     ).astype(jnp.bfloat16)
     rows_in = rows_in.reshape(dp_count, held, CAP, D)
     experts = jnp.arange(EXPERTS, dtype=jnp.int32)
-    named = jnp.any(routes[:, :, None] == experts[None, None, :], axis=1)
+    named = jnp.any(all_routes[:, :, None] == experts[None, None, :], axis=1)
     sigmoid_vals = jax.nn.sigmoid(logits) * named.astype(jnp.float32)
-    route_weight = sigmoid_vals / jnp.sum(sigmoid_vals, axis=1, keepdims=True)
-    all_weights = lax.all_gather(route_weight, "dp", axis=0, tiled=True)
+    all_weights = sigmoid_vals / jnp.sum(sigmoid_vals, axis=1, keepdims=True)
     outs = []
     for index in range(held):
         rows = rows_in[:, index].reshape(dp_count * CAP, D)

time: 376 us -> 376 us (level)
  blocking collectives: 69.2 us -> 50 us
  matrix products: 59.5 us -> 74.9 us
  Pallas kernels: 164 us -> 168 us
    all_gather x3 -> x1, blocking collectives: 32.7 us -> 13.9 us  [local(): router_and_gain = lax.all_gather(router_and_gain, 'mp', axis=0, tiled=True)]
    dot_general x1, matrix products: 2.28 us -> 17.8 us  [local(): jnp.dot(scaled, all_router, precision=lax.Precision.HIGHEST) * inverse]
    pallas_call x2, Pallas kernels: 118 us -> 122 us  [gather_blocks(): pl.pallas_call(gather_kernel, out_shape=jax.ShapeDtypeStruct((dp_count *...]
where the time goes in v4:
time: 376 us; the launch traced here: 369 us
  Pallas kernels  168 us (45%)
  matrix products  74.9 us (20%)
  blocking collectives  50 us (13%)
  other arithmetic  38.5 us (10%)
  between operations  14.2 us (4%)
  local copies, waits for them, and re-layouts  12.8 us (3%)
  starting transfers between devices  7.99 us (2%)
    pallas_call x2, Pallas kernels, gather_blocks(): pl.pallas_call(gather_kernel, out_shape=jax.ShapeDtypeStruct((dp_count *...  122 us
    pallas_call x1, Pallas kernels, scatter_sum(): pl.pallas_call(scatter_kernel, out_shape=jax.ShapeDtypeStruct(block, jnp....  46.1 us
    dot_general x2, matrix products, local(): jnp.dot(hidden, down_local[low:high], preferred_element_type=jnp.float32)  20.7 us
    all_gather x1, blocking collectives, local(): all_routes = lax.all_gather(routes, 'dp', axis=0, tiled=True)  18.4 us
    dot_general x1, matrix products, local(): jnp.dot(scaled, all_router, precision=lax.Precision.HIGHEST) * inverse  17.8 us
    all_to_all x1, blocking collectives, local(): lax.all_to_all(attended.reshape(local_heads, tok_rows, HEAD_DIM), 'dp', s...  17.7 us
    all_gather x1, blocking collectives, local(): router_and_gain = lax.all_gather(router_and_gain, 'mp', axis=0, tiled=True)  13.9 us
    dot_general x2, matrix products, local(): jnp.dot(rows, gate_local[:, low:high], preferred_element_type=jnp.float32)  10.5 us
  transfers between devices with their start and end apart: 3, of which 1 were waited for; matrix products, arithmetic and copies ran while one was open for 10% of the time, Pallas kernels for 20%

profile of v4, /device:TPU:0, one launch (start us, length us, event | category | flops | bytes accessed | tf_op | source)
XLA Modules:
  0.0 369.4 jit_solution(3543272647305704565)
XLA Ops:
  10.4 1.5 broadcast_in_dim.34
  11.9 7.4 %all-to-all-start = ((bf16[16,128,384]{2,1,0:T(8,128)(2,1)}), bf16[16,128,384]{2,1,0:T(8,128)(2,1)S(1)}, u32[]{:S(2)}, u32[]{:S(2)}) async-start(bf16[16,128,384]{2,1,0:T(8,128)(2,1)} %bitcast.10), calls=%async_computation | async-start | bytes 3145728 | tf_op jit(solution)/shard_map/all_to_all | solution.py:498
  19.8 75.4 %gather_blocks.2 = bf16[2048,2048]{1,0:T(8,128)(2,1)} custom-call(bf16[128,1024]{1,0:T(8,128)(2,1)} %block_ref.1), custom_call_target="tpu_custom_call" | custom-call | tf_op jit(solution)/shard_map/gather_blocks/pallas_call | solution.py:183
  95.2 2.8 multiply_sine_fusion.1
  99.3 3.7 multiply_cosine_fusion
  103.0 5.3 %fusion.3 = f32[2048]{0:T(1024)S(1)} fusion(bf16[2048,2048]{1,0:T(8,128)(2,1)} %gather_blocks.2), kind=kLoop, calls=%fused_computation.7 | loop fusion | flops 12580864 | bytes 8396800 | tf_op jit(solution)/shard_map/reduce_sum | solution.py:507
  108.3 4.1 %fusion.7 = f32[2048,384]{0,1:T(8,128)S(1)} fusion(bf16[2048,384]{1,0:T(8,128)(2,1)S(1)} %bitcast.95, bf16[2048,2048]{1,0:T(8,128)(2,1)S(1)} %copy-done.1, f32[2048]{0:T(1024)S(1)} %copy-done.17, f32[2048]{0:T(1024)S(1)} %add_rsqrt_fusion.2), kind=kOutput, calls=%fused_computation.11 | convolution fusion | flops 3238002688 | bytes 13123584 | tf_op jit(solution)/shard_map/dot_general | solution.py:523
  112.5 1.5 copy-done.2
  114.0 1.2 fusion.74
  115.3 1.9 reshape.368
  117.1 1.7 constant_dynamic-slice_fusion
  120.7 1.3 fusion.85
  122.0 3.4 fusion.22
  125.5 4.8 %fusion.26 = f32[1024]{0:T(1024)S(1)} fusion(f32[1024,2048]{1,0:T(8,128)S(1)} %get-tuple-element.26, f32[1024]{0:T(1024)S(1)} %get-tuple-element.25, s32[1024]{0:T(1024)S(1)} %bitcast.110, pred[2048]{0:T(1024)(128)(4,1)S(1)} %broadcast_compare_fusion, s32[2048]{0:T(1024)S(1)} %convert_reduce_fusion, s32[1024]{0:T(1024)S(1)} %bitcast.113), kind=kLoop, calls=%fused_computation.30 | loop fusion | flops 18873344 | bytes 8415232 | tf_op jit(solution)/shard_map/reduce_sum | solution.py:459
  130.3 3.9 %fusion.71 = bf16[1024,128]{1,0:T(8,128)(2,1)S(1)} fusion(f32[1024,2048]{1,0:T(8,128)S(1)} %get-tuple-element.26, f32[1024]{0:T(1024)S(1)} %get-tuple-element.25, f32[2048,384]{0,1:T(8,128)S(1)} %copy-done.3, f32[1024]{0:T(1024)S(1)} %fusion.26, s32[1024]{0:T(1024)S(1)} %bitcast.111, s32[2048]{0:T(1024)S(1)} %convert_reduce_fusion, s32[1024]{0:T(1024)S(1)} %bitcast.114, ...), kind=kOutput, calls=%fused_computation.76 | convolution fusion | flops 556007424 | bytes 9201664 | tf_op jit(solution)/shard_map/dot_general | solution.py:460
  134.4 17.7 %all_to_all.10 = bf16[8,128,128]{1,2,0:T(8,128)(2,1)S(1)} all-to-all(bf16[8,128,128]{1,2,0:T(8,128)(2,1)S(1)} %copy.50), channel_id=1, replica_groups={{0,4,8,12,16,20,24,28},{2,6,10,14,18,22,26,30},{1,5,9,13,17,21,25,29},{..., dimensions={0} | all-to-all | bytes 524288 | tf_op jit(solution)/shard_map/all_to_all | solution.py:533
  152.1 2.6 all-gather.2.cloned.1.call-done
  154.7 3.9 %fusion.104 = f32[128,2048]{1,0:T(8,128)} fusion(bf16[128,1024]{0,1:T(8,128)(2,1)S(1)} %bitcast.99, bf16[1024,2048]{1,0:T(8,128)(2,1)} %all-gather.2.cloned.1.call-done), kind=kOutput, calls=%fused_computation.142 | convolution fusion | flops 536870912 | bytes 5505024 | tf_op jit(solution)/shard_map/dot_general | solution.py:542
  158.7 13.9 %all_gather.11 = f32[2048,65]{0,1:T(8,128)S(1)} all-gather(f32[1024,65]{0,1:T(8,128)S(1)} %pad_maximum_fusion.2), channel_id=1, replica_groups=mesh['dp'=16,'mp'=2] {'mp'}, dimensions={0}, use_global_device_ids=true | all-gather | bytes 798720 | tf_op jit(solution)/shard_map/all_gather | solution.py:511
  172.6 18.4 %all_gather.10 = s32[2048,8]{0,1:T(8,128)S(1)} all-gather(s32[128,8]{0,1:T(8,128)S(1)} %copy-done.14), channel_id=1, replica_groups=mesh['dp'=16,'mp'=2] {'dp'}, dimensions={0}, use_global_device_ids=true | all-gather | bytes 69632 | tf_op jit(solution)/shard_map/all_gather | solution.py:509
  192.3 1.8 add_convert_fusion.1.block_ref
  194.1 46.8 %gather_blocks.3 = bf16[2048,2048]{1,0:T(8,128)(2,1)} custom-call(bf16[128,1024]{1,0:T(8,128)(2,1)} %add_convert_fusion.1.block_ref), custom_call_target="tpu_custom_call" | custom-call | tf_op jit(solution)/shard_map/gather_blocks/pallas_call | solution.py:183
  240.8 5.2 %fusion.6 = f32[2048]{0:T(1024)S(1)} fusion(bf16[2048,2048]{1,0:T(8,128)(2,1)} %gather_blocks.3), kind=kLoop, calls=%fused_computation.10 | loop fusion | flops 12580864 | bytes 8396800 | tf_op jit(solution)/shard_map/reduce_sum | solution.py:547
  246.6 17.8 %fusion.103 = (f32[2048]{0:T(1024)S(1)}, f32[2048,64]{0,1:T(8,128)S(1)}) fusion(pred[2048,64]{0,1:T(8,128)(4,1)S(1)} %fusion.44, f32[2048]{0:T(1024)S(1)} %add_rsqrt_fusion, f32[2048,65]{0,1:T(8,128)S(1)} %all_gather.11, bf16[2048,2048]{1,0:T(8,128)(2,1)S(1)} %copy-done, f32[2048]{0:T(1024)S(1)} %bitcast.107), kind=kOutput, calls=%fused_computation.141 | convolution fusion | flops 3230398464 | bytes 9592832 | tf_op jit(solution)/shard_map/dot_general | solution.py:550
  264.7 8.5 %fusion.2 = bf16[2048,2048]{1,0:T(8,128)(2,1)} fusion(bf16[2048,2048]{1,0:T(8,128)(2,1)} %gather_blocks.3, f32[2048]{0:T(1024)S(1)} %add_rsqrt_fusion, f32[2048]{0:T(1024)S(1)} %bitcast.108), kind=kLoop, calls=%fused_computation.6 | loop fusion | flops 16777216 | bytes 16793600 | tf_op jit(solution)/shard_map/convert_element_type | solution.py:549
  273.2 4.6 %convolution_convert_fusion = bf16[16,64,2048]{2,1,0:T(8,128)(2,1)S(1)} fusion(pred[16,64,128]{2,1,0:T(32,128)(4,1)S(1)} %bitcast_compare_fusion, bf16[16,128,2048]{2,1,0:T(8,128)(2,1)} %bitcast.86), kind=kOutput, calls=%fused_computation.49 | convolution fusion | flops 538968064 | bytes 12713984 | tf_op jit(solution)/shard_map/dot_general | solution.py:579
  278.3 6.8 %fusion.30 = f32[512,1024]{1,0:T(8,128)} fusion(bf16[512,2048]{1,0:T(8,128)(2,1)S(1)} %bitcast.93, bf16[2048,2048]{1,0:T(8,128)(2,1)} %bitcast.117), kind=kOutput, calls=%fused_computation.34 | convolution fusion | flops 2147483648 | bytes 8388608 | tf_op jit(solution)/shard_map/dot_general | solution.py:594
  285.2 3.7 fusion.34
  288.8 10.6 %fusion.48 = bf16[512,2048]{1,0:T(8,128)(2,1)} fusion(bf16[1,2048,2048]{2,1,0:T(8,128)(2,1)} %param.31, f32[512,1024]{1,0:T(8,128)} %fusion.30, bf16[512,2048]{1,0:T(8,128)(2,1)} %bitcast.94, bf16[2048,2048]{1,0:T(8,128)(2,1)} %bitcast.121), kind=kOutput, calls=%fused_computation.51 | convolution fusion | flops 4299161600 | bytes 14680064 | tf_op jit(solution)/shard_map/dot_general | solution.py:597
  299.4 10.1 %fusion.45 = bf16[512,2048]{1,0:T(8,128)(2,1)} fusion(bf16[1,2048,2048]{2,1,0:T(8,128)(2,1)} %param.31, f32[512,1024]{1,0:T(8,128)} %fusion.34, bf16[512,2048]{1,0:T(8,128)(2,1)S(1)} %bitcast.92, bf16[2048,2048]{1,0:T(8,128)(2,1)} %bitcast.122), kind=kOutput, calls=%fused_computation.50 | convolution fusion | flops 4299161600 | bytes 14680064 | tf_op jit(solution)/shard_map/dot_general | solution.py:597
  309.6 5.8 %fusion.23 = bf16[16,128,2048]{2,1,0:T(8,128)(2,1)S(1)} fusion(bf16[16,128,128]{2,1,0:T(8,128)(2,1)S(1)} %bitcast.101, bf16[16,32,2048]{2,1,0:T(8,128)(2,1)} %bitcast.124, bf16[16,32,2048]{2,1,0:T(8,128)(2,1)} %bitcast.125), kind=kOutput, calls=%fused_computation.29 | convolution fusion | flops 1111490560 | bytes 13107200 | tf_op jit(solution)/shard_map/dot_general | solution.py:610
  315.4 46.1 %scatter_sum.1 = f32[128,1024]{1,0:T(8,128)S(1)} custom-call(bf16[2048,2048]{1,0:T(8,128)(2,1)S(1)} %bitcast.85), custom_call_target="tpu_custom_call" | custom-call | tf_op jit(solution)/shard_map/scatter_sum/pallas_call | solution.py:414
  (93 shorter events, 10.9 us)
Async XLA Ops:
  6.5 12.8 %copy-start.18 = (s32[4]{0:T(128)S(1)}, s32[4]{0:T(128)}, u32[]{:S(2)}) copy-start(s32[4]{0:T(128)} %param.17) | copy-start | bytes 52
  9.9 85.2 %copy-start.12 = (s32[2048]{0:T(1024)S(1)}, s32[2048]{0:T(1024)}, u32[]{:S(2)}) copy-start(s32[2048]{0:T(1024)} %param.18) | copy-start | bytes 24580
  11.9 86.2 %all-to-all-start = ((bf16[16,128,384]{2,1,0:T(8,128)(2,1)}), bf16[16,128,384]{2,1,0:T(8,128)(2,1)S(1)}, u32[]{:S(2)}, u32[]{:S(2)}) async-start(bf16[16,128,384]{2,1,0:T(8,128)(2,1)} %bitcast.10), calls=%async_computation | async-start | bytes 3145728 | tf_op jit(solution)/shard_map/all_to_all | solution.py:498
  19.3 135.4 %all-gather.2.cloned.1.call-start = ((), (), s32[]{:S(2)}) async-start(), calls=%async_computation.3 | async-start | bytes 4456448 | tf_op jit(solution)/shard_map/all_gather | solution.py:504
  19.8 88.5 %copy-start.17 = (f32[2048]{0:T(1024)S(1)}, f32[2048]{0:T(1024)}, u32[]{:S(2)}) copy-start(f32[2048]{0:T(1024)} %param.20) | copy-start | bytes 24580
  98.0 1.2 copy-start.6
  98.1 94.2 %reduce-scatter.2.cloned.1.call-start = ((), (), s32[]{:S(2)}) async-start(), calls=%async_computation.4 | async-start | bytes 1572864 | tf_op jit(solution)/shard_map/reduce_scatter | solution.py:543
  98.6 9.6 %copy-start.1 = (bf16[2048,2048]{1,0:T(8,128)(2,1)S(1)}, bf16[2048,2048]{1,0:T(8,128)(2,1)}, u32[]{:S(2)}) copy-start(bf16[2048,2048]{1,0:T(8,128)(2,1)} %gather_blocks.2) | copy-start | bytes 25165828
  99.3 9.0 %copy-start.7 = (bf16[16,128,384]{2,1,0:T(8,128)(2,1)S(1)}, bf16[16,128,384]{2,1,0:T(8,128)(2,1)}, u32[]{:S(2)}) copy-start(bf16[16,128,384]{2,1,0:T(8,128)(2,1)} %copy-done.6) | copy-start | bytes 4718596
  108.3 5.7 %copy-start.16 = (f32[128]{0:T(128)S(1)}, f32[128]{0:T(128)}, u32[]{:S(2)}) copy-start(f32[128]{0:T(128)} %param.23) | copy-start | bytes 1540
  112.4 1.7 copy-start.2
  112.4 7.3 %copy-start.15 = (f32[128]{0:T(128)S(1)}, f32[128]{0:T(128)}, u32[]{:S(2)}) copy-start(f32[128]{0:T(128)} %param.22) | copy-start | bytes 1540
  119.4 2.6 copy-start.3
  119.4 2.6 copy-start.9
  119.4 2.6 copy-start.10
  130.3 28.4 %copy-start.11 = (f32[1024,64]{0,1:T(8,128)S(1)}, f32[1024,64]{0,1:T(8,128)}, u32[]{:S(2)}) copy-start(f32[1024,64]{0,1:T(8,128)} %param.28) | copy-start | bytes 786436
  130.3 28.4 %copy-start.13 = (f32[1024]{0:T(1024)S(1)}, f32[1024]{0:T(1024)}, u32[]{:S(2)}) copy-start(f32[1024]{0:T(1024)} %param.21) | copy-start | bytes 12292
  134.2 38.4 %copy-start.14 = (s32[128,8]{0,1:T(8,128)S(1)}, s32[128,8]{0,1:T(8,128)}, u32[]{:S(2)}) copy-start(s32[128,8]{0,1:T(8,128)} %param.19) | copy-start | bytes 12292
  134.2 58.1 %copy-start.8 = (bf16[128,1024]{1,0:T(8,128)(2,1)S(1)}, bf16[128,1024]{1,0:T(8,128)(2,1)}, u32[]{:S(2)}) copy-start(bf16[128,1024]{1,0:T(8,128)(2,1)} %block_ref.1) | copy-start | bytes 786436
  240.8 5.8 %copy-start = (bf16[2048,2048]{1,0:T(8,128)(2,1)S(1)}, bf16[2048,2048]{1,0:T(8,128)(2,1)}, u32[]{:S(2)}) copy-start(bf16[2048,2048]{1,0:T(8,128)(2,1)} %gather_blocks.3) | copy-start | bytes 25165828
  277.9 7.3 %slice-start = ((s8[8388608]{0:T(1024)(128)(4,1)}), s8[4194304]{0:T(1024)(128)(4,1)S(1)}, s32[]{:S(2)}) async-start(s8[8388608]{0:T(1024)(128)(4,1)} %bitcast.118), calls=%async_computation.5 | async-start | bytes 8388608
  278.3 10.6 %copy-start.5 = (bf16[16,1,32,2048]{3,2,1,0:T(8,128)(2,1)}, bf16[16,1,32,2048]{3,2,1,0:T(8,128)(2,1)S(1)}, u32[]{:S(2)}) copy-start(bf16[16,1,32,2048]{3,2,1,0:T(8,128)(2,1)S(1)} %get-tuple-element.12) | copy-start | bytes 6291460
  278.3 6.9 %slice-start.1 = ((s8[8388608]{0:T(1024)(128)(4,1)}), s8[4194304]{0:T(1024)(128)(4,1)S(1)}, s32[]{:S(2)}) async-start(s8[8388608]{0:T(1024)(128)(4,1)} %bitcast.118), calls=%async_computation.6 | async-start | bytes 8388608
  315.4 46.2 %copy-start.4 = (bf16[128,1024]{1,0:T(8,128)(2,1)S(1)}, bf16[128,1024]{1,0:T(8,128)(2,1)}, u32[]{:S(2)}) copy-start(bf16[128,1024]{1,0:T(8,128)(2,1)} %add_convert_fusion.1.block_ref) | copy-start | bytes 786436
Sparse Core Ops, SparseCore 0:
  98.2 56.4 all-gather.1
  158.7 22.1 reduce-scatter.1
